TPU v7x, 32 devices: a whole 2x2x4 slice. The times are simulated.
32 devices in a mesh: dp: 8 (over z, x), tensor: 4 (over y, core).
Axes of the slice: x: 2, y: 2, z: 4, core: 2. Of those that a mesh axis runs over, the one named last changes fastest.
Arguments:
- hidden_in: bfloat16 [16384, 2560], P('dp'), may hold values from -6 to 6
- segment_ids: int32 [8, 2048], P('dp'), may hold values from 0 to 3, as said below
- positions: int32 [8, 2048], P('dp'), may hold values from 0 to 4095, as said below
- cotangent: bfloat16 [16384, 2560], P('dp'), may hold values from -6 to 6
- query_weight: bfloat16 [2560, 2048], P('dp', 'tensor'), may hold values from -0.125 to 0.125
- key_projection: bfloat16 [2560, 1024], P('dp', 'tensor'), may hold values from -0.125 to 0.125
- value_projection: bfloat16 [2560, 1024], P('dp', 'tensor'), may hold values from -0.125 to 0.125
- output_weight: bfloat16 [2048, 2560], P('tensor', 'dp'), may hold values from -0.125 to 0.125
- gate_weight: bfloat16 [2560, 10240], P('dp', 'tensor'), may hold values from -0.125 to 0.125
- upward_weight: bfloat16 [2560, 10240], P('dp', 'tensor'), may hold values from -0.125 to 0.125
- down_weight: bfloat16 [10240, 2560], P('tensor', 'dp'), may hold values from -0.0625 to 0.0625
- norm_gains: bfloat16 [4, 2560], P(None, 'dp'), may hold values from -0.8984375 to 0.8984375
- head_gains: bfloat16 [2, 256], P(None, 'dp'), may hold values from -0.8984375 to 0.8984375
- query_mean: float32 [2560, 2048], P('dp', 'tensor'), may hold values from -6 to 6
- query_square: float32 [2560, 2048], P('dp', 'tensor'), may hold values from 1 to 100
- key_first_moment: float32 [2560, 1024], P('dp', 'tensor'), may hold values from -6 to 6
- key_second_moment: float32 [2560, 1024], P('dp', 'tensor'), may hold values from 1 to 100
- value_first_moment: float32 [2560, 1024], P('dp', 'tensor'), may hold values from -6 to 6
- value_second_moment: float32 [2560, 1024], P('dp', 'tensor'), may hold values from 1 to 100
- output_mean: float32 [2048, 2560], P('tensor', 'dp'), may hold values from -6 to 6
- output_square: float32 [2048, 2560], P('tensor', 'dp'), may hold values from 1 to 100
- gate_mean: float32 [2560, 10240], P('dp', 'tensor'), may hold values from -6 to 6
- gate_square: float32 [2560, 10240], P('dp', 'tensor'), may hold values from 1 to 100
- upward_mean: float32 [2560, 10240], P('dp', 'tensor'), may hold values from -6 to 6
- upward_square: float32 [2560, 10240], P('dp', 'tensor'), may hold values from 1 to 100
- down_mean: float32 [10240, 2560], P('tensor', 'dp'), may hold values from -6 to 6
- down_square: float32 [10240, 2560], P('tensor', 'dp'), may hold values from 1 to 100
- norms_mean: float32 [4, 2560], P(None, 'dp'), may hold values from -6 to 6
- norms_square: float32 [4, 2560], P(None, 'dp'), may hold values from 1 to 100
- heads_mean: float32 [2, 256], P(None, 'dp'), may hold values from -6 to 6
- heads_square: float32 [2, 256], P(None, 'dp'), may hold values from 1 to 100
Outputs:
- block_output: bfloat16 [16384, 2560], P('dp')
- input_gradient: float32 [16384, 2560], P('dp')
- query_gradient: float32 [2560, 2048], P('dp', 'tensor')
- key_gradient: float32 [2560, 1024], P('dp', 'tensor')
- value_gradient: float32 [2560, 1024], P('dp', 'tensor')
- output_gradient: float32 [2048, 2560], P('tensor', 'dp')
- gate_gradient: float32 [2560, 10240], P('dp', 'tensor')
- upward_gradient: float32 [2560, 10240], P('dp', 'tensor')
- down_gradient: float32 [10240, 2560], P('tensor', 'dp')
- norms_gradient: float32 [4, 2560], P(None, 'dp')
- heads_gradient: float32 [2, 256], P(None, 'dp')
- query_updated: float32 [2560, 2048], P('dp', 'tensor')
- key_updated: float32 [2560, 1024], P('dp', 'tensor')
- value_updated: float32 [2560, 1024], P('dp', 'tensor')
- output_updated: float32 [2048, 2560], P('tensor', 'dp')
- gate_updated: float32 [2560, 10240], P('dp', 'tensor')
- upward_updated: float32 [2560, 10240], P('dp', 'tensor')
- down_updated: float32 [10240, 2560], P('tensor', 'dp')
- norms_updated: float32 [4, 2560], P(None, 'dp')
- heads_updated: float32 [2, 256], P(None, 'dp')
- query_newmean: float32 [2560, 2048], P('dp', 'tensor')
- key_newmean: float32 [2560, 1024], P('dp', 'tensor')
- value_newmean: float32 [2560, 1024], P('dp', 'tensor')
- output_newmean: float32 [2048, 2560], P('tensor', 'dp')
- gate_newmean: float32 [2560, 10240], P('dp', 'tensor')
- upward_newmean: float32 [2560, 10240], P('dp', 'tensor')
- down_newmean: float32 [10240, 2560], P('tensor', 'dp')
- norms_newmean: float32 [4, 2560], P(None, 'dp')
- heads_newmean: float32 [2, 256], P(None, 'dp')
- query_newsquare: float32 [2560, 2048], P('dp', 'tensor')
- key_newsquare: float32 [2560, 1024], P('dp', 'tensor')
- value_newsquare: float32 [2560, 1024], P('dp', 'tensor')
- output_newsquare: float32 [2048, 2560], P('tensor', 'dp')
- gate_newsquare: float32 [2560, 10240], P('dp', 'tensor')
- upward_newsquare: float32 [2560, 10240], P('dp', 'tensor')
- down_newsquare: float32 [10240, 2560], P('tensor', 'dp')
- norms_newsquare: float32 [4, 2560], P(None, 'dp')
- heads_newsquare: float32 [2, 256], P(None, 'dp')
Inputs may be any that keep to these rules, and one draw needn't show every extreme that they name: `segment_ids`: in each row, ids never fall and every id of 0 to 3 names one or more tokens. Within a document, positions rise by one from token to token; each row's first document starts at 0.
All inputs are finite; a program needn't handle non-finite values.
Results may differ from a plain program's by a relative error of at most 0.038.
Values may be sent and summed in bfloat16 or wider, within the bound.
No kernel may reach another device: no remote copies, remote signals or barrier semaphores. Data moves between devices by JAX's collectives and lax.ppermute only.
A program may use at most 448 MiB of HBM per device.

v0:
```python
import functools

import jax
import jax.numpy as jnp
from jax import lax
from jax.experimental import pallas as pl
from jax.experimental.pallas import tpu as pltpu
from jax.sharding import PartitionSpec as P

HEAD_WIDTH = 256
WINDOW = 1024
STEP = 4
CHUNKS = 2
BLOCK = 256

NORM_EPS = 1e-06
BETA_ONE = 0.9
BETA_TWO = 0.999
ADAM_EPS = 1e-08
LEARN_RATE = 0.01
DECAY_RATE = 0.1
ROPE_BASE = 10000.0
GELU_COEF = 0.7978845608028654
MASKED = -1e30


DP = "dp"
TENSOR = "tensor"
F32 = jnp.float32
HALF = jnp.bfloat16


def contract(a, b, form):
    dims = ((0 if form[0] == "t" else 1,), (1 if form[1] == "t" else 0,))
    return lax.dot_general(a, b, (dims, ((), ())), preferred_element_type=F32)


def mm(a, b):
    return contract(a, b, "nn")


def mm_nt(a, b):
    return contract(a, b, "nt")


def fused_dots(grid, terms, extras, outs, finish):
    arrays, specs, plan, flops = [], [], [], 0
    steps = 1
    for size in grid:
        steps *= size
    for left, left_spec, right, right_spec, form, slot in terms:
        plan.append((len(arrays), form, slot))
        arrays += [left, right]
        specs += [left_spec, right_spec]
        shape = [n for n in left_spec.block_shape if n is not None]
        other = [n for n in right_spec.block_shape if n is not None]
        columns = other[0] if form[1] == "t" else other[1]
        flops += 2 * steps * shape[0] * shape[1] * columns
    base = len(arrays)
    for extra, spec in extras:
        arrays.append(extra)
        specs.append(spec)
    count = len(arrays)
    slots = 1 + max(slot for _, _, slot in plan)

    def kernel(*refs):
        sums = [None] * slots
        for at, form, slot in plan:
            product = contract(refs[at][...], refs[at + 1][...], form)
            sums[slot] = product if sums[slot] is None else sums[slot] + product
        finish(sums, refs[base:count], refs[count:])

    moved = sum(a.size * a.dtype.itemsize for a in {id(a): a for a in arrays}.values())
    return pl.pallas_call(
        kernel,
        grid=grid,
        in_specs=specs,
        out_specs=[spec for _, _, spec in outs],
        out_shape=[jax.ShapeDtypeStruct(shape, dtype) for shape, dtype, _ in outs],
        compiler_params=pltpu.CompilerParams(
            dimension_semantics=("arbitrary",) * len(grid),
            vmem_limit_bytes=56 * 1024 * 1024,
        ),
        cost_estimate=pl.CostEstimate(flops=flops, bytes_accessed=moved, transcendentals=0),
    )(*arrays)


def rope_tables(places, head_size):
    half_dim = head_size // 2
    frequency = ROPE_BASE ** (-2.0 * jnp.arange(half_dim, dtype=F32) / head_size)
    angles = places.astype(F32)[:, None] * frequency[None, :]
    return (jnp.cos(angles), jnp.sin(angles))


def rotate(values, cosine, sine_table):
    half_dim = values.shape[-1] // 2
    first_half = values[..., :half_dim]
    second_half = values[..., half_dim:]
    return jnp.concatenate(
        [
            first_half * cosine - second_half * sine_table,
            second_half * cosine + first_half * sine_table,
        ],
        axis=-1,
    )


def rms_unit(values):
    factor = lax.rsqrt(jnp.mean(values * values, axis=-1, keepdims=True) + NORM_EPS)
    return (values * factor, factor)


def rms_backward(upstream, normed, factor, gain_row):
    scaled = upstream * (1.0 + gain_row)
    return factor * (scaled - normed * jnp.mean(scaled * normed, axis=-1, keepdims=True))


def gelu_parts(values):
    tangent = jnp.tanh(GELU_COEF * (values + 0.044715 * values * values * values))
    value = 0.5 * values * (1.0 + tangent)
    slope = 0.5 * (1.0 + tangent) + 0.5 * values * (1.0 - tangent * tangent) * GELU_COEF * (
        1.0 + 3.0 * 0.044715 * values * values
    )
    return (value, slope)


def row_sum(values, width):
    total = sum(jnp.sum(v, axis=-1, keepdims=True) for v in values)
    return total / width


def unit_of(values, width):
    factor = lax.rsqrt(row_sum([v * v for v in values], width) + NORM_EPS)
    return ([v * factor for v in values], factor)


def back_of(upstream, units, factor, gains, width):
    scaled = [e * (1.0 + g) for e, g in zip(upstream, gains)]
    mean = row_sum([s * u for s, u in zip(scaled, units)], width)
    return [factor * (s - u * mean) for s, u in zip(scaled, units)]


def halves(ref):
    return [ref[w].astype(F32) for w in range(ref.shape[0])]


def put(ref, pair):
    for w, value in enumerate(pair):
        ref[w] = value.astype(ref.dtype)


def put_sum(ref, upstream, units):
    @pl.when(pl.program_id(0) == 0)
    def _():
        ref[...] = jnp.zeros_like(ref)

    for w, (e, u) in enumerate(zip(upstream, units)):
        ref[w] += jnp.sum(e * u, axis=0, keepdims=True)


def glue(inputs, gains, outs, sums, body):
    rows, half = inputs[0].shape[1:]
    tile = min(64, rows)
    block = lambda n: pl.BlockSpec((n, tile, half), lambda i: (0, i, 0))
    still = pl.BlockSpec((2, 1, half), lambda i: (0, 0, 0))
    return pl.pallas_call(
        body,
        grid=(rows // tile,),
        in_specs=[block(x.shape[0]) for x in inputs] + [still] * len(gains),
        out_specs=[block(2)] * len(outs) + [still] * sums,
        out_shape=[jax.ShapeDtypeStruct((2, rows, half), dtype) for dtype in outs]
        + [jax.ShapeDtypeStruct((2, 1, half), F32)] * sums,
        compiler_params=kernel_params(),
        cost_estimate=pl.CostEstimate(
            flops=64 * rows * half, bytes_accessed=40 * rows * half, transcendentals=0
        ),
    )(*inputs, *gains)


def glue_one(mine, near, own, gain_two, gain_three, sum_ref, middle_ref, ffn_ref):
    width = 2 * mine.shape[2]
    total = [a + b for a, b in zip(halves(mine), halves(near))]
    units, _ = unit_of(total, width)
    middle = [x + u * (1.0 + g) for x, u, g in zip(halves(own), units, halves(gain_two))]
    units, _ = unit_of(middle, width)
    put(sum_ref, total)
    put(middle_ref, middle)
    put(ffn_ref, [u * (1.0 + g) for u, g in zip(units, halves(gain_three))])


def glue_two(
    mine_a, near_a, mine_b, near_b, middle, upstream, gain, block_ref, grad_ref, sum_ref
):
    width = 2 * middle.shape[2]
    total = [mine_a[0] + near_a[0].astype(F32), mine_b[0] + near_b[0].astype(F32)]
    units, factor = unit_of(total, width)
    gains = halves(gain)
    errors = halves(upstream)
    put(block_ref, [x + u * (1.0 + g) for x, u, g in zip(halves(middle), units, gains)])
    put(grad_ref, back_of(errors, units, factor, gains, width))
    put_sum(sum_ref, errors, units)


def glue_three(
    mine, near, middle, upstream, attn_sum, gain_two, gain_three,
    grad_ref, attn_ref, sum_three_ref, sum_two_ref,
):
    width = 2 * middle.shape[2]
    errors = [a + b for a, b in zip(halves(mine), halves(near))]
    units, factor = unit_of(halves(middle), width)
    back = back_of(errors, units, factor, halves(gain_three), width)
    put_sum(sum_three_ref, errors, units)
    grads = [x + y for x, y in zip(halves(upstream), back)]
    put(grad_ref, grads)
    units, factor = unit_of(halves(attn_sum), width)
    put_sum(sum_two_ref, grads, units)
    put(attn_ref, back_of(grads, units, factor, halves(gain_two), width))


def glue_four(mine, near, own, middle_grad, gain_one, out_ref, sum_ref):
    width = 2 * own.shape[2]
    errors = [a + b for a, b in zip(halves(mine), halves(near))]
    units, factor = unit_of(halves(own), width)
    back = back_of(errors, units, factor, halves(gain_one), width)
    put(out_ref, [x + y for x, y in zip(halves(middle_grad), back)])
    put_sum(sum_ref, errors, units)


def take_piece(refs, per, store):
    for k, ref in enumerate(refs):

        @pl.when(pl.program_id(0) // per == k)
        def _(ref=ref):
            store(ref)


def piece_index(per, k):
    return lambda i: jnp.clip(i - k * per, 0, per - 1)


def place_rows(pieces, order, dtype):
    rows, width = pieces[0].shape
    tile = min(128, rows)
    per = rows // tile

    def kernel(order_ref, *refs):
        def store(ref):
            refs[-1][...] = ref[...].astype(dtype)

        take_piece(refs[:-1], per, store)

    specs = [
        pl.BlockSpec((tile, width), lambda i, o, k=k: (piece_index(per, k)(i), 0))
        for k in range(len(pieces))
    ]
    return pl.pallas_call(
        kernel,
        grid_spec=pltpu.PrefetchScalarGridSpec(
            num_scalar_prefetch=1,
            grid=(len(pieces) * per,),
            in_specs=specs,
            out_specs=pl.BlockSpec((tile, width), lambda i, o: (o[i // per] * per + i % per, 0)),
        ),
        out_shape=jax.ShapeDtypeStruct((len(pieces) * rows, width), dtype),
        compiler_params=kernel_params(),
        cost_estimate=pl.CostEstimate(flops=0, bytes_accessed=24 * rows * width, transcendentals=0),
    )(order, *pieces)


def all_rows(pieces, weights, width, extras, outs, finish, first=0, order=None):
    rows, half = pieces[0].shape[1:]
    tile = min(256, rows)
    per = rows // tile
    steps = len(pieces) * per
    count = len(pieces)
    slots = len(weights)

    def kernel(*refs):
        if order is not None:
            refs = refs[1:]
        flat = refs[count : count + 2 * slots]
        rest = refs[count + 2 * slots :]
        if count > 1:
            rest, left = rest[:-1], rest[-1]

            def store(ref):
                left[...] = ref[...]

            take_piece(refs[:count], per, store)
        else:
            left = refs[0]
        sums = [
            contract(left[0], flat[2 * s][...], "nn") + contract(left[1], flat[2 * s + 1][...], "nn")
            for s in range(slots)
        ]
        finish(sums, rest[: len(extras)], rest[len(extras) :])

    specs = [
        pl.BlockSpec((2, tile, half), lambda i, *o, k=k: (0, piece_index(per, k)(i), 0))
        for k in range(count)
    ]
    for pair in weights:
        columns = min(pair[0].shape[1], width)
        specs += [pl.BlockSpec((half, columns), lambda i, *o: (0, 0))] * 2
    skip = first * (rows // tile)
    specs += [pl.BlockSpec((tile, width), lambda i, *o: (skip + i, 0))] * len(extras)
    if order is None:
        target = pl.BlockSpec((tile, width), lambda i: (i, 0))
    else:
        target = pl.BlockSpec((tile, width), lambda i, o: (o[i // per] * per + i % per, 0))
    scratch = [pltpu.VMEM((2, tile, half), HALF)] if count > 1 else []
    arrays = list(pieces) + [w for pair in weights for w in pair] + list(extras)
    return pl.pallas_call(
        kernel,
        grid_spec=pltpu.PrefetchScalarGridSpec(
            num_scalar_prefetch=0 if order is None else 1,
            grid=(steps,),
            in_specs=specs,
            out_specs=[target] * len(outs),
            scratch_shapes=scratch,
        ),
        out_shape=[jax.ShapeDtypeStruct((steps * tile, width), dtype) for dtype in outs],
        compiler_params=pltpu.CompilerParams(
            dimension_semantics=("arbitrary",), vmem_limit_bytes=56 * 1024 * 1024
        ),
        cost_estimate=pl.CostEstimate(
            flops=4 * steps * tile * half * sum(pair[0].shape[1] for pair in weights),
            bytes_accessed=sum(a.size * a.dtype.itemsize for a in arrays),
            transcendentals=0,
        ),
    )(*([] if order is None else [order]), *arrays)


def visible(lo_ref, start, span, heads):
    rows = lax.broadcasted_iota(jnp.int32, (span, BLOCK), 0) + start
    queries = lax.broadcasted_iota(jnp.int32, (1, BLOCK), 1) + pl.program_id(0) * BLOCK
    seen = (rows >= lo_ref[...]) & (rows <= queries)
    return jnp.concatenate([seen] * heads, axis=1)


def stacked(ref, heads):
    width = ref.shape[1] // heads
    return jnp.concatenate([ref[:, h * width : (h + 1) * width] for h in range(heads)], axis=0)


def row_of(ref, heads):
    return jnp.concatenate([ref[h : h + 1, :] for h in range(heads)], axis=1)


def key_start(span):
    end = (pl.program_id(0) + 1) * BLOCK
    return pl.multiple_of(jnp.maximum(end - span, 0), BLOCK)


def attend_kernel(span, heads, q_ref, k_ref, vt_ref, lo_ref, out_ref, lse_ref):
    start = key_start(span)
    width = k_ref.shape[1]
    queries = stacked(q_ref, heads)
    scores = mm_nt(k_ref[pl.ds(start, span), :], queries)
    scores = jnp.where(visible(lo_ref, start, span, heads), scores, MASKED)
    top = jnp.max(scores, axis=0, keepdims=True)
    weights = jnp.exp(scores - top)
    total = jnp.sum(weights, axis=0, keepdims=True)
    result = mm(vt_ref[:, pl.ds(start, span)], weights.astype(HALF)) / total
    lse = top + jnp.log(total)
    for h in range(heads):
        part = slice(h * BLOCK, (h + 1) * BLOCK)
        out_ref[:, h * width : (h + 1) * width] = result[:, part].T.astype(HALF)
        lse_ref[h : h + 1, :] = lse[:, part]


def attend_back_kernel(
    span, heads, q_ref, k_ref, kt_ref, v_ref, do_ref, lo_ref, lse_ref, out_ref,
    dq_ref, dk_ref, dv_ref,
):
    start = key_start(span)
    width = k_ref.shape[1]

    @pl.when(pl.program_id(0) == 0)
    def _():
        dk_ref[...] = jnp.zeros_like(dk_ref)
        dv_ref[...] = jnp.zeros_like(dv_ref)

    keys = pl.ds(start, span)
    queries = stacked(q_ref, heads)
    upstream = stacked(do_ref, heads)
    scores = mm_nt(k_ref[keys, :], queries)
    scores = jnp.where(visible(lo_ref, start, span, heads), scores, MASKED)
    weights = jnp.exp(scores - row_of(lse_ref, heads))
    dv_ref[keys, :] += mm(weights.astype(HALF), upstream)
    weight_grad = mm_nt(v_ref[keys, :], upstream)
    pull = upstream.astype(F32) * stacked(out_ref, heads).astype(F32)
    delta = jnp.sum(pull.T, axis=0, keepdims=True)
    score_grad = (weights * (weight_grad - delta)).astype(HALF)
    dk_ref[keys, :] += mm(score_grad, queries)
    grad = mm(kt_ref[:, keys], score_grad)
    for h in range(heads):
        dq_ref[:, h * width : (h + 1) * width] = grad[:, h * BLOCK : (h + 1) * BLOCK].T


def kernel_params():
    return pltpu.CompilerParams(
        dimension_semantics=("arbitrary",), vmem_limit_bytes=48 * 1024 * 1024
    )


def full_spec(shape):
    return pl.BlockSpec(shape, lambda i: (0,) * len(shape))


def attend(q, k, v, lo):
    length, columns = q.shape
    width = k.shape[1]
    heads = columns // width
    span = min(WINDOW + BLOCK, length)
    rows = pl.BlockSpec((BLOCK, columns), lambda i: (i, 0))
    lane = lambda n: pl.BlockSpec((n, BLOCK), lambda i: (0, i))
    steps = length // BLOCK
    return pl.pallas_call(
        functools.partial(attend_kernel, span, heads),
        grid=(steps,),
        in_specs=[rows, full_spec(k.shape), full_spec((width, length)), lane(1)],
        out_specs=[rows, lane(heads)],
        out_shape=[
            jax.ShapeDtypeStruct(q.shape, HALF),
            jax.ShapeDtypeStruct((heads, length), F32),
        ],
        compiler_params=kernel_params(),
        cost_estimate=pl.CostEstimate(
            flops=4 * steps * span * BLOCK * columns,
            bytes_accessed=4 * length * columns + 4 * length * width,
            transcendentals=steps * span * BLOCK * heads,
        ),
        name="attend",
    )(q, k, v.T, lo)


def attend_back(q, k, v, do, lo, lse, out):
    length, columns = q.shape
    width = k.shape[1]
    heads = columns // width
    span = min(WINDOW + BLOCK, length)
    rows = pl.BlockSpec((BLOCK, columns), lambda i: (i, 0))
    lane = lambda n: pl.BlockSpec((n, BLOCK), lambda i: (0, i))
    steps = length // BLOCK
    return pl.pallas_call(
        functools.partial(attend_back_kernel, span, heads),
        grid=(steps,),
        in_specs=[
            rows, full_spec(k.shape), full_spec((width, length)), full_spec(v.shape), rows,
            lane(1), lane(heads), rows,
        ],
        out_specs=[rows, full_spec(k.shape), full_spec(v.shape)],
        out_shape=[
            jax.ShapeDtypeStruct(q.shape, F32),
            jax.ShapeDtypeStruct(k.shape, F32),
            jax.ShapeDtypeStruct(v.shape, F32),
        ],
        compiler_params=kernel_params(),
        cost_estimate=pl.CostEstimate(
            flops=10 * steps * span * BLOCK * columns,
            bytes_accessed=8 * length * columns + 14 * length * width,
            transcendentals=steps * span * BLOCK * heads,
        ),
        name="attend_back",
    )(q, k, k.T, v, do, lo, lse, out)


def first_visible(segments):
    length = segments.shape[0]
    ids = jnp.arange(length, dtype=jnp.int32)
    begins = jnp.concatenate([jnp.ones((1,), bool), segments[1:] != segments[:-1]])
    starts = lax.cummax(jnp.where(begins, ids, 0), axis=0)
    return jnp.maximum(starts, ids - (WINDOW - 1))[None, :]


def adam_update(weight_shard, grad_shard, mean_shard, square_shard, decay):
    new_mean = BETA_ONE * mean_shard + (1.0 - BETA_ONE) * grad_shard
    new_square = BETA_TWO * square_shard + (1.0 - BETA_TWO) * grad_shard * grad_shard
    mean_hat = new_mean / (1.0 - BETA_ONE**STEP)
    square_hat = new_square / (1.0 - BETA_TWO**STEP)
    weight_value = weight_shard.astype(F32)
    updated = weight_value - LEARN_RATE * (
        mean_hat / (jnp.sqrt(square_hat) + ADAM_EPS) + decay * weight_value
    )
    return (updated, new_mean, new_square)


def step(
    n_dp,
    hidden_in,
    segment_ids,
    positions,
    cotangent,
    query_weight,
    key_projection,
    value_projection,
    output_weight,
    gate_weight,
    upward_weight,
    down_weight,
    norm_gains,
    head_gains,
    query_mean,
    query_square,
    key_first_moment,
    key_second_moment,
    value_first_moment,
    value_second_moment,
    output_mean,
    output_square,
    gate_mean,
    gate_square,
    upward_mean,
    upward_square,
    down_mean,
    down_square,
    norms_mean,
    norms_square,
    heads_mean,
    heads_square,
):
    tokens, model = hidden_in.shape
    share = model // n_dp
    quarter = tokens // 4
    half = model // 2
    spot = lax.axis_index(DP)
    parity = spot % 2
    place = lax.axis_index(TENSOR)
    core = place % 2
    row = place // 2
    outer = [[2 * i + p for i in range(n_dp // 2)] for p in range(2)]
    twins = [(i, i ^ 1) for i in range(n_dp)]

    def to_twin(x):
        return lax.ppermute(x, DP, twins)

    def to_core(x):
        return lax.ppermute(x, TENSOR, [(i, i ^ 1) for i in range(4)])

    def to_row(x):
        return lax.ppermute(x, TENSOR, [(i, i ^ 2) for i in range(4)])

    def split_columns(x):
        parts = [x[:, i * share : (i + 1) * share] for i in range(n_dp)]
        even = jnp.concatenate(parts[0::2], axis=1)
        odd = jnp.concatenate(parts[1::2], axis=1)
        mine = jnp.where(parity == 0, even, odd)
        return jnp.stack([mine, jnp.where(parity == 0, odd, even)])

    def join_columns(pair):
        even = jnp.where(parity == 0, pair[0], pair[1])
        odd = jnp.where(parity == 0, pair[1], pair[0])
        parts = []
        for i in range(n_dp // 2):
            parts.append(even[:, i * share : (i + 1) * share])
            parts.append(odd[:, i * share : (i + 1) * share])
        return jnp.concatenate(parts, axis=1)

    order = [
        (core * 2 + row) * quarter,
        ((1 - core) * 2 + row) * quarter,
        (core * 2 + 1 - row) * quarter,
        ((1 - core) * 2 + 1 - row) * quarter,
    ]

    def rows_at(x, at):
        return lax.dynamic_slice_in_dim(x, at, quarter, x.ndim - 2)

    def own_order(x):
        return jnp.concatenate([rows_at(x, at) for at in order], axis=0)

    def quarter_of(arrays, which):
        per = 4 // len(arrays)
        return (arrays[which // per], which % per)

    def product(pieces, weights, which, added, dtype, parts=(0, 1)):
        tile = 256 if half % 256 == 0 else half
        out = pl.BlockSpec((len(parts), quarter, tile), lambda i: (0, 0, i))
        terms = []
        for slot, w in enumerate(parts):
            for (left, column, depth), right in zip(pieces, weights):
                array, at = quarter_of(left, which)
                terms.append(
                    (
                        array,
                        pl.BlockSpec(
                            (quarter, depth), lambda i, at=at, column=column: (at, column)
                        ),
                        right[w],
                        pl.BlockSpec((tile, depth), lambda i: (i, 0)),
                        "nt",
                        slot,
                    )
                )

        def finish(sums, extras, outs):
            for slot, total in enumerate(sums):
                for extra in extras:
                    total = total + extra[slot].astype(F32)
                outs[0][slot] = total.astype(dtype)

        return fused_dots(
            (half // tile,),
            terms,
            [(extra, out) for extra in added],
            [((len(parts), quarter, half), dtype, out)],
            finish,
        )[0]

    def reduce_rows(pieces, weights, parts=(0, 1), early={}):

        def one(which, added, dtype):
            lefts, rights = pieces, weights
            if which in early:
                lefts, rights = pieces[-1:], weights[-1:]
                added = [early[which]] + added
            return product(lefts, rights, which, added, dtype, parts)

        far_in = to_core(one(3, [], HALF))
        near_in = to_row(one(2, [far_in], HALF))
        side_in = to_core(one(1, [], HALF))
        return (one(0, [side_in], F32), near_in)

    def spread(x):
        across = to_row(x)
        return [x, to_core(x), across, to_core(across)]

    def gather_outer(piece):
        return lax.all_gather(piece, DP, axis=0, tiled=True, axis_index_groups=outer)

    def gather_model(shard, chunks):
        width = shard.shape[1] // chunks
        found = []
        for j in range(chunks):
            mine = gather_outer(shard[:, j * width : (j + 1) * width])
            found.append((mine, to_twin(mine)))
        return found

    def weight_grad(left, right, which, added):
        right, column, width = right
        tile = 256 if half % 256 == 0 else half
        out = pl.BlockSpec((tile, width), lambda i: (i, 0))
        parts = 1 if len(left) == len(right) == 1 else 4
        rows = tokens // parts
        terms = []
        for p in range(parts):
            piece, at = quarter_of(left, p) if parts > 1 else (left[0], 0)
            other, there = quarter_of(right, p) if parts > 1 else (right[0], 0)
            terms.append(
                (
                    piece,
                    pl.BlockSpec((None, rows, tile), lambda i, at=at: (which, at, i)),
                    other,
                    pl.BlockSpec((rows, width), lambda i, there=there: (there, column)),
                    "tn",
                    0,
                )
            )

        def finish(sums, extras, outs):
            total = sums[0]
            for extra in extras:
                total = total + extra[...].astype(F32)
            outs[0][...] = total.astype(HALF)

        return fused_dots(
            (half // tile,),
            terms,
            [(extra, out) for extra in added],
            [((half, width), HALF, out)],
            finish,
        )[0]

    def scatter_model(left, rights):
        found = []
        for right in rights:
            other = to_twin(weight_grad(left, right, 1, []))
            total = weight_grad(left, right, 0, [other])
            found.append(
                lax.psum_scatter(
                    total, DP, scatter_dimension=0, tiled=True, axis_index_groups=outer
                )
            )
        return jnp.concatenate(found, axis=1) if len(found) > 1 else found[0]

    q_cols = query_weight.shape[1]
    kv_cols = key_projection.shape[1]
    front_width = q_cols + 2 * kv_cols
    gain_block = jnp.concatenate(
        [
            norm_gains.T,
            jnp.pad(head_gains.T, ((0, share - head_gains.shape[1]), (0, 0))),
            jnp.zeros((share, 128 - 6), HALF),
        ],
        axis=1,
    )
    front_shard = jnp.concatenate(
        [query_weight, key_projection, value_projection, gain_block], axis=1
    )
    front = gather_model(front_shard, 1)[0]
    back = gather_model(output_weight.T, 1)[0]
    gates = gather_model(gate_weight, CHUNKS)
    upwards = gather_model(upward_weight, CHUNKS)
    down_shard = down_weight.T
    units = down_weight.shape[0]
    downs = gather_model(down_shard[:, : units // 2], 1)
    for at, tag in ((units // 2, "down1"), (3 * units // 4, "down2")):
        piece = down_shard[:, at : at + units // 4]
        if tag == "down1":
            mine = gather_outer(piece)
            downs.append((mine, to_twin(mine)))
        else:
            twin_piece = to_twin(piece)
            downs.append((gather_outer(piece), gather_outer(twin_piece)))

    gains = jnp.stack([f[:, front_width : front_width + 4].T for f in front]).astype(F32)
    gain = [gains[:, i : i + 1, :] for i in range(4)]
    head_width = head_gains.shape[1]
    head_parts = [
        f[:, front_width + 4 : front_width + 6]
        .reshape(n_dp // 2, share, 2)[:, :head_width, :]
        .astype(F32)
        for f in front
    ]
    head_even = jnp.where(parity == 0, head_parts[0], head_parts[1])
    head_odd = jnp.where(parity == 0, head_parts[1], head_parts[0])
    head_gain = jnp.stack([head_even, head_odd], axis=1).reshape(n_dp * head_width, 2).T

    whole = lambda arrays: (arrays, 0, arrays[0].shape[1])
    rows_pair = split_columns(hidden_in)
    upstream = split_columns(rows_at(cotangent, order[0]))
    rows_pair, upstream = lax.optimization_barrier((rows_pair, upstream))
    rows_f32 = rows_pair.astype(F32)
    factor_all = lax.rsqrt(jnp.mean(rows_f32 * rows_f32, axis=(0, 2), keepdims=True) + NORM_EPS)
    attn_in = (rows_f32 * factor_all * (1.0 + gain[0])).astype(HALF)
    own_in = rows_at(rows_pair, order[0])

    def keep(sums, extras, outs):
        outs[0][...] = sums[0].astype(outs[0].dtype)

    projected = all_rows([attn_in], [front], front_width, [], [F32], keep)[0]
    cosine, sine_table = rope_tables(positions[0], HEAD_WIDTH)
    scale = HEAD_WIDTH ** (-0.5)
    heads = [projected[:, i : i + HEAD_WIDTH] for i in range(0, q_cols + kv_cols, HEAD_WIDTH)]
    queries = q_cols // HEAD_WIDTH
    head_row = lambda i: head_gain[0 if i < queries else 1][None, :]
    head_units, factors, turned = [], [], []
    for i, values in enumerate(heads):
        unit, factor = rms_unit(values)
        head_units.append(unit)
        factors.append(factor)
        turned.append(rotate(unit * (1.0 + head_row(i)), cosine, sine_table).astype(HALF))
    query_scaled = jnp.concatenate([t * HALF(scale) for t in turned[:queries]], axis=1)
    key_heads = jnp.concatenate(turned[queries:], axis=1)
    value_heads = projected[:, q_cols + kv_cols :].astype(HALF)
    lo = first_visible(segment_ids[0])
    attended, lse = attend(query_scaled, key_heads, value_heads, lo)
    attended_own = own_order(attended)
    mine, near = reduce_rows([whole([attended_own])], [back])
    attn_sum, middle, ffn_in = glue(
        [mine, near, own_in], [gain[1], gain[2]], [F32, F32, HALF], 0, glue_one
    )
    ffn_pieces = spread(ffn_in)

    def act(sums, extras, outs):
        value, slope = gelu_parts(sums[0])
        outs[0][...] = (value * sums[1]).astype(HALF)
        outs[1][...] = value.astype(HALF)
        outs[2][...] = (slope * sums[1]).astype(HALF)

    mixed, kept_value, kept_slope = [], [], []
    for j in range(CHUNKS):
        made = all_rows(
            ffn_pieces, [gates[j], upwards[j]], gates[j][0].shape[1], [], [HALF] * 3, act
        )
        mixed.append([made[0]])
        kept_value.append(made[1])
        kept_slope.append(made[2])

    half_units = units // 2
    hidden_parts = [
        (mixed[0], 0, half_units),
        (mixed[1], 1, half_units // 2),
        (mixed[1], 0, half_units // 2),
    ]
    ordered = [downs[0], downs[2], downs[1]]
    mine_a, near_a = reduce_rows(hidden_parts, ordered, (0,))
    early = {q: product(hidden_parts[:-1], ordered[:-1], q, [], F32, (1,)) for q in (3, 2)}
    mine_b, near_b = reduce_rows(hidden_parts, ordered, (1,), early)
    block_pair, ffn_grad, gain_four = glue(
        [mine_a, near_a, mine_b, near_b, middle, upstream], [gain[3]], [HALF, HALF], 1, glue_two
    )

    grad_pieces = spread(ffn_grad)
    down_wgrad = scatter_model(grad_pieces, [hidden_parts[0], hidden_parts[2], hidden_parts[1]])

    def hidden(sums, extras, outs):
        at = 0
        for total in sums:
            part = slice(at, at + total.shape[1])
            outs[0][:, part] = (total * extras[0][:, part].astype(F32)).astype(HALF)
            outs[1][:, part] = (total * extras[1][:, part].astype(F32)).astype(HALF)
            at += total.shape[1]

    gate_back, upward_back = [], []
    for j in range(CHUNKS):
        made = [
            all_rows(
                grad_pieces[2 * p : 2 * p + 2],
                downs[:1] if j == 0 else downs[1:],
                half_units,
                [kept_slope[j], kept_value[j]],
                [HALF] * 2,
                hidden,
                first=2 * p,
            )
            for p in range(2)
        ]
        gate_back.append([m[0] for m in made])
        upward_back.append([m[1] for m in made])

    mine, near = reduce_rows([whole(a) for a in gate_back + upward_back], gates + upwards)
    gate_wgrad = scatter_model(ffn_pieces, [whole(a) for a in gate_back])
    upward_wgrad = scatter_model(ffn_pieces, [whole(a) for a in upward_back])
    middle_grad, attn_grad, gain_three, gain_two = glue(
        [mine, near, middle, upstream, attn_sum], [gain[1], gain[2]], [F32, HALF], 2, glue_three
    )
    attn_pieces = spread(attn_grad)
    spots = jnp.stack(order).astype(jnp.int32) // quarter
    block_output = place_rows(spread(join_columns(block_pair)), spots, HALF)

    grad_natural = all_rows(attn_pieces, [back], q_cols, [], [HALF], keep, order=spots)[0]
    query_grad, key_grad, value_grad = attend_back(
        query_scaled, key_heads, value_heads, grad_natural, lo, lse, attended
    )
    output_wgrad = scatter_model(attn_pieces, [whole([attended_own])])
    flats, sums = [], []
    for i, (unit, factor) in enumerate(zip(head_units, factors)):
        at = i * HEAD_WIDTH if i < queries else (i - queries) * HEAD_WIDTH
        source = query_grad * scale if i < queries else key_grad
        back_turned = rotate(source[:, at : at + HEAD_WIDTH], cosine, -sine_table)
        sums.append(jnp.sum(back_turned * unit, axis=0))
        flats.append(rms_backward(back_turned, unit, factor, head_row(i)).astype(HALF))
    head_part = jnp.stack([sum(sums[:queries]), sum(sums[queries:])])
    front_grad = jnp.concatenate(flats + [value_grad.astype(HALF)], axis=1)
    front_own = own_order(front_grad)
    mine, near = reduce_rows([whole([front_own])], [front])
    front_wgrad = scatter_model([attn_in], [whole([front_grad])])
    input_pair, gain_one = glue([mine, near, own_in, middle_grad], [gain[0]], [HALF], 1, glue_four)
    input_grad = place_rows(spread(join_columns(input_pair)), spots, F32)

    gain_rows = join_columns(jnp.concatenate([gain_one, gain_two, gain_three, gain_four], axis=1))
    flat = jnp.concatenate([gain_rows.reshape(-1), head_part.reshape(-1)]).reshape(-1, 128)
    flat = flat + to_core(flat)
    flat = flat + to_row(flat)
    step_bit = 1
    while step_bit < n_dp:
        swap = [(i, i ^ step_bit) for i in range(n_dp)]
        flat = flat + lax.ppermute(flat, DP, swap)
        step_bit *= 2
    flat = flat.reshape(-1)
    gain_total = flat[: 4 * model].reshape(4, model)
    head_total = flat[4 * model :].reshape(2, -1)
    norms_grad = lax.dynamic_slice_in_dim(gain_total, spot * share, share, 1)
    heads_grad = lax.dynamic_slice_in_dim(head_total, spot * head_width, head_width, 1)

    grad_shards = (
        front_wgrad[:, :q_cols].astype(F32),
        front_wgrad[:, q_cols : q_cols + kv_cols].astype(F32),
        front_wgrad[:, q_cols + kv_cols :].astype(F32),
        output_wgrad.T.astype(F32),
        gate_wgrad.astype(F32),
        upward_wgrad.astype(F32),
        down_wgrad.T.astype(F32),
        norms_grad,
        heads_grad,
    )
    params = (
        query_weight,
        key_projection,
        value_projection,
        output_weight,
        gate_weight,
        upward_weight,
        down_weight,
        norm_gains,
        head_gains,
    )
    means = (
        query_mean,
        key_first_moment,
        value_first_moment,
        output_mean,
        gate_mean,
        upward_mean,
        down_mean,
        norms_mean,
        heads_mean,
    )
    squares = (
        query_square,
        key_second_moment,
        value_second_moment,
        output_square,
        gate_square,
        upward_square,
        down_square,
        norms_square,
        heads_square,
    )
    decays = (DECAY_RATE,) * 7 + (0.0, 0.0)
    results = [
        adam_update(param, grad_item, mean_item, square_item, decay)
        for param, grad_item, mean_item, square_item, decay in zip(
            params, grad_shards, means, squares, decays
        )
    ]
    updated = tuple((item[0] for item in results))
    new_means = tuple((item[1] for item in results))
    new_squares = tuple((item[2] for item in results))
    return (block_output, input_grad) + grad_shards + updated + new_means + new_squares


def shards(n_dp, *arrays):
    return step(n_dp, *arrays)


def solution(mesh):
    in_specs = (
        P(DP, None),
        P(DP, None),
        P(DP, None),
        P(DP, None),
        P(DP, TENSOR),
        P(DP, TENSOR),
        P(DP, TENSOR),
        P(TENSOR, DP),
        P(DP, TENSOR),
        P(DP, TENSOR),
        P(TENSOR, DP),
        P(None, DP),
        P(None, DP),
        P(DP, TENSOR),
        P(DP, TENSOR),
        P(DP, TENSOR),
        P(DP, TENSOR),
        P(DP, TENSOR),
        P(DP, TENSOR),
        P(TENSOR, DP),
        P(TENSOR, DP),
        P(DP, TENSOR),
        P(DP, TENSOR),
        P(DP, TENSOR),
        P(DP, TENSOR),
        P(TENSOR, DP),
        P(TENSOR, DP),
        P(None, DP),
        P(None, DP),
        P(None, DP),
        P(None, DP),
    )
    out_specs = (
        P(DP, None),
        P(DP, None),
        P(DP, TENSOR),
        P(DP, TENSOR),
        P(DP, TENSOR),
        P(TENSOR, DP),
        P(DP, TENSOR),
        P(DP, TENSOR),
        P(TENSOR, DP),
        P(None, DP),
        P(None, DP),
        P(DP, TENSOR),
        P(DP, TENSOR),
        P(DP, TENSOR),
        P(TENSOR, DP),
        P(DP, TENSOR),
        P(DP, TENSOR),
        P(TENSOR, DP),
        P(None, DP),
        P(None, DP),
        P(DP, TENSOR),
        P(DP, TENSOR),
        P(DP, TENSOR),
        P(TENSOR, DP),
        P(DP, TENSOR),
        P(DP, TENSOR),
        P(TENSOR, DP),
        P(None, DP),
        P(None, DP),
        P(DP, TENSOR),
        P(DP, TENSOR),
        P(DP, TENSOR),
        P(TENSOR, DP),
        P(DP, TENSOR),
        P(DP, TENSOR),
        P(TENSOR, DP),
        P(None, DP),
        P(None, DP),
    )
    return jax.shard_map(
        functools.partial(shards, mesh.shape[DP]),
        mesh=mesh,
        in_specs=in_specs,
        out_specs=out_specs,
        check_vma=False,
    )
```

profile of v0, /device:TPU:0, one launch (start us, length us, event | category | flops | bytes accessed | tf_op | source)
XLA Modules:
  0.0 1899.7 jit_solution(12857514497518579040)
XLA Ops:
  110.4 36.2 %collective-permute-done = bf16[1280,1152]{0,1:T(8,128)(2,1)} collective-permute-done((bf16[1280,1152]{0,1:T(8,128)(2,1)}, bf16[1280,1152]{0,1:T(8,128)(2,1)}, u32[]{:S(2)}, u32[]{:S(2)}) %collective-permute-start) | collective-permute-done | bytes 2949152 | tf_op jit(solution)/shard_map/ppermute | solution.py:536
  164.7 17.0 shard_map.590
  202.1 13.7 attend.1
  255.2 44.9 %collective-permute-done.4.near = bf16[2,512,1280]{2,1,0:T(8,128)(2,1)S(1)} collective-permute-done((bf16[2,512,1280]{2,1,0:T(8,128)(2,1)}, bf16[2,512,1280]{2,1,0:T(8,128)(2,1)S(1)}, u32[]{:S(2)}, u32[]{:S(2)}) %collective-permute-start.4) | collective-permute-done | bytes 2621472 | tf_op jit(solution)/shard_map/ppermute | solution.py:542
  317.2 54.6 %collective-permute-done.6.refs_2_.refs_4_ = bf16[2,512,1280]{2,1,0:T(8,128)(2,1)} collective-permute-done((bf16[2,512,1280]{2,1,0:T(8,128)(2,1)S(1)}, bf16[2,512,1280]{2,1,0:T(8,128)(2,1)}, u32[]{:S(2)}, u32[]{:S(2)}) %collective-permute-start.6) | collective-permute-done | bytes 2621472 | tf_op jit(solution)/shard_map/ppermute | solution.py:542
  373.4 92.7 %collective-permute-done.16 = bf16[320,640]{1,0:T(8,128)(2,1)S(1)} collective-permute-done((bf16[320,640]{1,0:T(8,128)(2,1)S(1)}, bf16[320,640]{1,0:T(8,128)(2,1)S(1)}, u32[]{:S(2)}, u32[]{:S(2)}) %collective-permute-start.16) | collective-permute-done | bytes 409632 | tf_op jit(solution)/shard_map/ppermute | solution.py:536
  479.0 38.5 %shard_map.597 = (bf16[2048,1280]{1,0:T(8,128)(2,1)}, bf16[2048,1280]{1,0:T(8,128)(2,1)}, bf16[2048,1280]{1,0:T(8,128)(2,1)}) custom-call(bf16[2,512,1280]{2,1,0:T(8,128)(2,1)} %copy-done, bf16[2,512,1280]{2,1,0:T(8,128)(2,1)} %collective-permute-done.5.refs_1_.refs_2_, bf16[2,512,1280]{2,1,0:T(8,128)(2,1)} %collective-permute-done.6.refs_2_.refs_4_, ...), custom_call_target="tpu_custom_call" | custom-call | flops 26843545600 | bytes 23592960 | tf_op jit(solution)/shard_map/pallas_call | solution.py:313
  517.6 22.7 %collective-permute-done.9.refs_7_.refs_13_ = bf16[1280,1280]{1,0:T(8,128)(2,1)} collective-permute-done((bf16[1280,1280]{1,0:T(8,128)(2,1)}, bf16[1280,1280]{1,0:T(8,128)(2,1)}, u32[]{:S(2)}, u32[]{:S(2)}) %collective-permute-start.9) | collective-permute-done | bytes 3276832 | tf_op jit(solution)/shard_map/ppermute | solution.py:536
  540.2 70.2 %collective-permute-done.8.refs_5_.refs_9_ = bf16[1280,1280]{1,0:T(8,128)(2,1)} collective-permute-done((bf16[1280,1280]{1,0:T(8,128)(2,1)}, bf16[1280,1280]{1,0:T(8,128)(2,1)}, u32[]{:S(2)}, u32[]{:S(2)}) %collective-permute-start.8) | collective-permute-done | bytes 3276832 | tf_op jit(solution)/shard_map/ppermute | solution.py:536
  610.5 37.9 %shard_map.596 = (bf16[2048,1280]{1,0:T(8,128)(2,1)}, bf16[2048,1280]{1,0:T(8,128)(2,1)}, bf16[2048,1280]{1,0:T(8,128)(2,1)}) custom-call(bf16[2,512,1280]{2,1,0:T(8,128)(2,1)} %copy-done, bf16[2,512,1280]{2,1,0:T(8,128)(2,1)} %collective-permute-done.5.refs_1_.refs_2_, bf16[2,512,1280]{2,1,0:T(8,128)(2,1)} %collective-permute-done.6.refs_2_.refs_4_, ...), custom_call_target="tpu_custom_call" | custom-call | flops 26843545600 | bytes 23592960 | tf_op jit(solution)/shard_map/pallas_call | solution.py:313
  656.9 56.2 %collective-permute-done.15.refs_1_.refs_3_ = bf16[1280,1280]{1,0:T(8,128)(2,1)} collective-permute-done((bf16[1280,1280]{1,0:T(8,128)(2,1)}, bf16[1280,1280]{1,0:T(8,128)(2,1)}, u32[]{:S(2)}, u32[]{:S(2)}) %collective-permute-start.15) | collective-permute-done | bytes 3276832 | tf_op jit(solution)/shard_map/ppermute | solution.py:536
  792.9 27.6 %collective-permute-done.20.near_b = bf16[1,512,1280]{2,1,0:T(8,128)(2,1)S(1)} collective-permute-done((bf16[1,512,1280]{2,1,0:T(8,128)(2,1)}, bf16[1,512,1280]{2,1,0:T(8,128)(2,1)S(1)}, u32[]{:S(2)}, u32[]{:S(2)}) %collective-permute-start.20) | collective-permute-done | bytes 1310752 | tf_op jit(solution)/shard_map/ppermute | solution.py:542
  832.1 58.0 %collective-permute-done.26.refs_0_.refs_4_ = bf16[2,512,1280]{2,1,0:T(8,128)(2,1)S(1)} collective-permute-done((bf16[2,512,1280]{2,1,0:T(8,128)(2,1)}, bf16[2,512,1280]{2,1,0:T(8,128)(2,1)S(1)}, u32[]{:S(2)}, u32[]{:S(2)}) %collective-permute-start.26) | collective-permute-done | bytes 2621472 | tf_op jit(solution)/shard_map/ppermute | solution.py:542
  906.7 36.6 %collective-permute-done.46.refs_8_ = bf16[1280,640]{1,0:T(8,128)(2,1)S(1)} collective-permute-done((bf16[1280,640]{1,0:T(8,128)(2,1)}, bf16[1280,640]{1,0:T(8,128)(2,1)S(1)}, u32[]{:S(2)}, u32[]{:S(2)}) %collective-permute-start.46) | collective-permute-done | bytes 1638432 | tf_op jit(solution)/shard_map/ppermute | solution.py:536
  975.7 25.2 %collective-permute-done.47.refs_8_ = bf16[1280,640]{1,0:T(8,128)(2,1)S(1)} collective-permute-done((bf16[1280,640]{1,0:T(8,128)(2,1)}, bf16[1280,640]{1,0:T(8,128)(2,1)S(1)}, u32[]{:S(2)}, u32[]{:S(2)}) %collective-permute-start.47) | collective-permute-done | bytes 1638432 | tf_op jit(solution)/shard_map/ppermute | solution.py:536
  1011.1 58.5 %collective-permute-done.45.refs_8_ = bf16[1280,1280]{1,0:T(8,128)(2,1)S(1)} collective-permute-done((bf16[1280,1280]{1,0:T(8,128)(2,1)}, bf16[1280,1280]{1,0:T(8,128)(2,1)S(1)}, u32[]{:S(2)}, u32[]{:S(2)}) %collective-permute-start.45) | collective-permute-done | bytes 3276832 | tf_op jit(solution)/shard_map/ppermute | solution.py:536
  1083.4 14.8 shard_map.611
  1098.2 14.7 shard_map.615
  1126.1 70.0 %collective-permute-done.42.refs_8_ = bf16[1280,1280]{1,0:T(8,128)(2,1)S(1)} collective-permute-done((bf16[1280,1280]{1,0:T(8,128)(2,1)}, bf16[1280,1280]{1,0:T(8,128)(2,1)S(1)}, u32[]{:S(2)}, u32[]{:S(2)}) %collective-permute-start.42) | collective-permute-done | bytes 3276832 | tf_op jit(solution)/shard_map/ppermute | solution.py:536
  1250.1 69.1 %collective-permute-done.41.refs_8_ = bf16[1280,1280]{1,0:T(8,128)(2,1)S(1)} collective-permute-done((bf16[1280,1280]{1,0:T(8,128)(2,1)}, bf16[1280,1280]{1,0:T(8,128)(2,1)S(1)}, u32[]{:S(2)}, u32[]{:S(2)}) %collective-permute-start.41) | collective-permute-done | bytes 3276832 | tf_op jit(solution)/shard_map/ppermute | solution.py:536
  1333.1 23.1 %shard_map.616 = bf16[2,512,1280]{2,1,0:T(8,128)(2,1)} custom-call(bf16[1024,1280]{1,0:T(8,128)(2,1)} %get-tuple-element.88.refs_0_.refs_8_.refs_5_.refs_7_, bf16[1280,1280]{1,0:T(8,128)(2,1)} %all-gather.15.cloned.1.call-done.refs_4_.refs_1_, bf16[1024,1280]{1,0:T(8,128)(2,1)} %get-tuple-element.89.refs_2_.refs_10_.refs_5_.refs_7_, ...), custom_call_target="tpu_custom_call" | custom-call | flops 13421772800 | bytes 36700160 | tf_op jit(solution)/shard_map/pallas_call | solution.py:74
  1369.6 22.7 %shard_map.612 = bf16[2,512,1280]{2,1,0:T(8,128)(2,1)} custom-call(bf16[1024,1280]{1,0:T(8,128)(2,1)} %get-tuple-element.82.refs_0_.refs_8_.refs_1_.refs_3_, bf16[1280,1280]{1,0:T(8,128)(2,1)} %all-gather.15.cloned.1.call-done.refs_4_.refs_1_, bf16[1024,1280]{1,0:T(8,128)(2,1)} %get-tuple-element.85.refs_2_.refs_10_.refs_1_.refs_3_, ...), custom_call_target="tpu_custom_call" | custom-call | flops 13421772800 | bytes 36700160 | tf_op jit(solution)/shard_map/pallas_call | solution.py:74
  1394.1 23.1 %shard_map.617 = bf16[2,512,1280]{2,1,0:T(8,128)(2,1)} custom-call(bf16[1024,1280]{1,0:T(8,128)(2,1)} %get-tuple-element.88.refs_0_.refs_8_.refs_5_.refs_7_, bf16[1280,1280]{1,0:T(8,128)(2,1)} %all-gather.15.cloned.1.call-done.refs_4_.refs_1_, bf16[1024,1280]{1,0:T(8,128)(2,1)} %get-tuple-element.89.refs_2_.refs_10_.refs_5_.refs_7_, ...), custom_call_target="tpu_custom_call" | custom-call | flops 13421772800 | bytes 39321600 | tf_op jit(solution)/shard_map/pallas_call | solution.py:74
  1417.3 24.1 %collective-permute-done.44.refs_8_ = bf16[1280,1280]{1,0:T(8,128)(2,1)S(1)} collective-permute-done((bf16[1280,1280]{1,0:T(8,128)(2,1)}, bf16[1280,1280]{1,0:T(8,128)(2,1)S(1)}, u32[]{:S(2)}, u32[]{:S(2)}) %collective-permute-start.44) | collective-permute-done | bytes 3276832 | tf_op jit(solution)/shard_map/ppermute | solution.py:536
  1455.3 23.2 %shard_map.613.mine = f32[2,512,1280]{2,1,0:T(8,128)} custom-call(bf16[1024,1280]{1,0:T(8,128)(2,1)} %get-tuple-element.82.refs_0_.refs_8_.refs_1_.refs_3_, bf16[1280,1280]{1,0:T(8,128)(2,1)} %all-gather.15.cloned.1.call-done.refs_4_.refs_1_, bf16[1024,1280]{1,0:T(8,128)(2,1)} %get-tuple-element.85.refs_2_.refs_10_.refs_1_.refs_3_, ...), custom_call_target="tpu_custom_call" | custom-call | flops 13421772800 | bytes 39321600 | tf_op jit(solution)/shard_map/pallas_call | solution.py:74
  1505.6 45.1 %collective-permute-done.31.refs_3_.refs_4_ = bf16[2,512,1280]{2,1,0:T(8,128)(2,1)} collective-permute-done((bf16[2,512,1280]{2,1,0:T(8,128)(2,1)}, bf16[2,512,1280]{2,1,0:T(8,128)(2,1)}, u32[]{:S(2)}, u32[]{:S(2)}) %collective-permute-start.31) | collective-permute-done | bytes 2621472 | tf_op jit(solution)/shard_map/ppermute | solution.py:542
  1588.8 14.1 shard_map.619.do_ref
  1603.0 21.0 %attend_back.1 = (f32[2048,512]{1,0:T(8,128)}, f32[2048,256]{1,0:T(8,128)S(1)}, f32[2048,256]{1,0:T(8,128)}) custom-call(bf16[2048,512]{1,0:T(8,128)(2,1)} %pad_maximum_fusion.4.q_ref, bf16[2048,256]{1,0:T(8,128)(2,1)S(1)} %copy-done.7, bf16[256,2048]{1,0:T(8,128)(2,1)S(1)} %copy-done.9, bf16[2048,256]{1,0:T(8,128)(2,1)S(1)} %copy-done.8, ...), custom_call_target="tpu_custom_call" | custom-call | flops 13421772800 | bytes 15728640 | tf_op jit(solution)/shard_map/attend_back/pallas_call | solution.py:446
  1710.1 14.2 shard_map.609
  1724.3 21.9 %collective-permute-done.39.refs_2_ = bf16[1280,1024]{1,0:T(8,128)(2,1)} collective-permute-done((bf16[1280,1024]{1,0:T(8,128)(2,1)}, bf16[1280,1024]{1,0:T(8,128)(2,1)}, u32[]{:S(2)}, u32[]{:S(2)}) %collective-permute-start.39) | collective-permute-done | bytes 2621472 | tf_op jit(solution)/shard_map/ppermute | solution.py:536
  1795.3 49.2 %collective-permute-done.49 = f32[84,128]{1,0:T(8,128)S(1)} collective-permute-done((f32[84,128]{1,0:T(8,128)S(1)}, f32[84,128]{1,0:T(8,128)S(1)}, u32[]{:S(2)}, u32[]{:S(2)}) %collective-permute-start.49) | collective-permute-done | bytes 43040 | tf_op jit(solution)/shard_map/ppermute | solution.py:542
  1877.2 15.5 shard_map.625
  (437 shorter events, 727.8 us)
Async XLA Ops:
  11.1 95.9 %all-gather.13.cloned.1.call-start = ((), (), s32[]{:S(2)}) async-start(), calls=%async_computation.10 | async-start | bytes 1638400 | tf_op jit(solution)/shard_map/all_gather | solution.py:630
  11.8 303.3 %all-gather.23.cloned.1.call-start = ((), (), s32[]{:S(2)}) async-start(), calls=%async_computation.15 | async-start | bytes 4096000 | tf_op jit(solution)/shard_map/all_gather | solution.py:630
  13.2 303.4 %all-gather.21.cloned.1.call-start = ((), (), s32[]{:S(2)}) async-start(), calls=%async_computation.14 | async-start | bytes 4096000 | tf_op jit(solution)/shard_map/all_gather | solution.py:630
  14.6 451.5 %all-gather.17.cloned.1.call-start = ((), (), s32[]{:S(2)}) async-start(), calls=%async_computation.12 | async-start | bytes 4096000 | tf_op jit(solution)/shard_map/all_gather | solution.py:630
  15.2 452.4 %all-gather.15.cloned.1.call-start = ((), (), s32[]{:S(2)}) async-start(), calls=%async_computation.11 | async-start | bytes 4096000 | tf_op jit(solution)/shard_map/all_gather | solution.py:630
  15.8 452.5 %all-gather.27.cloned.1.call-start = ((), (), s32[]{:S(2)}) async-start(), calls=%async_computation.17 | async-start | bytes 2048000 | tf_op jit(solution)/shard_map/all_gather | solution.py:630
  106.9 110.8 %collective-permute-start.1 = (bf16[1280,512]{1,0:T(8,128)(2,1)}, bf16[1280,512]{1,0:T(8,128)(2,1)S(1)}, u32[]{:S(2)}, u32[]{:S(2)}) collective-permute-start(bf16[1280,512]{1,0:T(8,128)(2,1)} %all-gather.13.cloned.1.call-done.refs_1_.refs_5_), channel_id=1, source_target_pairs={{0,4},{4,0},{8,12},{12,8},{16,20},{20,16},{24,28},{28,24},{1,5},{5... | collective-permute-start | bytes 3932168 | tf_op jit(solution)/shard_map/ppermute | solution.py:536
  226.0 251.5 %all-gather.19.cloned.1.call-start = ((), (), s32[]{:S(2)}) async-start(), calls=%async_computation.13 | async-start | bytes 4096000 | tf_op jit(solution)/shard_map/all_gather | solution.py:630
  243.6 404.8 %all-gather.25.cloned.1.call-start = ((), (), s32[]{:S(2)}) async-start(), calls=%async_computation.16 | async-start | bytes 2048000 | tf_op jit(solution)/shard_map/all_gather | solution.py:630
  315.2 152.5 %collective-permute-start.11 = (bf16[1280,1280]{1,0:T(8,128)(2,1)}, bf16[1280,1280]{1,0:T(8,128)(2,1)}, u32[]{:S(2)}, u32[]{:S(2)}) collective-permute-start(bf16[1280,1280]{1,0:T(8,128)(2,1)} %all-gather.23.cloned.1.call-done.refs_6_.refs_7_), channel_id=1, source_target_pairs={{0,4},{4,0},{8,12},{12,8},{16,20},{20,16},{24,28},{28,24},{1,5},{5... | collective-permute-start | bytes 9830408 | tf_op jit(solution)/shard_map/ppermute | solution.py:536
  316.6 151.6 %collective-permute-start.10 = (bf16[1280,1280]{1,0:T(8,128)(2,1)}, bf16[1280,1280]{1,0:T(8,128)(2,1)}, u32[]{:S(2)}, u32[]{:S(2)}) collective-permute-start(bf16[1280,1280]{1,0:T(8,128)(2,1)} %all-gather.21.cloned.1.call-done.refs_4_.refs_3_), channel_id=1, source_target_pairs={{0,4},{4,0},{8,12},{12,8},{16,20},{20,16},{24,28},{28,24},{1,5},{5... | collective-permute-start | bytes 9830408 | tf_op jit(solution)/shard_map/ppermute | solution.py:536
  317.2 160.4 %collective-permute-start.5 = (bf16[2,512,1280]{2,1,0:T(8,128)(2,1)S(1)}, bf16[2,512,1280]{2,1,0:T(8,128)(2,1)}, u32[]{:S(2)}, u32[]{:S(2)}) collective-permute-start(bf16[2,512,1280]{2,1,0:T(8,128)(2,1)S(1)} %get-tuple-element.73.refs_0_), channel_id=1, source_target_pairs={{0,1},{1,0},{2,3},{3,2},{4,5},{5,4},{6,7},{7,6},{8,9},{9,8},{10,11... | collective-permute-start | bytes 7864328 | tf_op jit(solution)/shard_map/ppermute | solution.py:539
  371.8 107.3 %collective-permute-start.7 = (bf16[2,512,1280]{2,1,0:T(8,128)(2,1)}, bf16[2,512,1280]{2,1,0:T(8,128)(2,1)}, u32[]{:S(2)}, u32[]{:S(2)}) collective-permute-start(bf16[2,512,1280]{2,1,0:T(8,128)(2,1)} %collective-permute-done.6.refs_2_.refs_4_), channel_id=1, source_target_pairs={{0,1},{1,0},{2,3},{3,2},{4,5},{5,4},{6,7},{7,6},{8,9},{9,8},{10,11... | collective-permute-start | bytes 7864328 | tf_op jit(solution)/shard_map/ppermute | solution.py:539
  371.8 285.0 %all-gather.29.cloned.1.call-start = ((), (), s32[]{:S(2)}) async-start(), calls=%async_computation.18 | async-start | bytes 2048000 | tf_op jit(solution)/shard_map/all_gather | solution.py:630
  371.9 94.3 %collective-permute-start.16 = (bf16[320,640]{1,0:T(8,128)(2,1)S(1)}, bf16[320,640]{1,0:T(8,128)(2,1)S(1)}, u32[]{:S(2)}, u32[]{:S(2)}) collective-permute-start(bf16[320,640]{1,0:T(8,128)(2,1)S(1)} %copy-done.28), channel_id=1, source_target_pairs={{0,4},{4,0},{8,12},{12,8},{16,20},{20,16},{24,28},{28,24},{1,5},{5... | collective-permute-start | bytes 1228808 | tf_op jit(solution)/shard_map/ppermute | solution.py:536
  467.6 142.8 %collective-permute-start.8 = (bf16[1280,1280]{1,0:T(8,128)(2,1)}, bf16[1280,1280]{1,0:T(8,128)(2,1)}, u32[]{:S(2)}, u32[]{:S(2)}) collective-permute-start(bf16[1280,1280]{1,0:T(8,128)(2,1)} %all-gather.15.cloned.1.call-done.refs_4_.refs_1_), channel_id=1, source_target_pairs={{0,4},{4,0},{8,12},{12,8},{16,20},{20,16},{24,28},{28,24},{1,5},{5... | collective-permute-start | bytes 9830408 | tf_op jit(solution)/shard_map/ppermute | solution.py:536
  468.2 1318.9 %reduce-scatter.24.cloned.1.call-start = ((), (), s32[]{:S(2)}) async-start(), calls=%async_computation.26 | async-start | bytes 2048000 | tf_op jit(solution)/shard_map/reduce_scatter | solution.py:681
  468.3 252.2 %collective-permute-start.17 = (bf16[1280,640]{1,0:T(8,128)(2,1)}, bf16[1280,640]{1,0:T(8,128)(2,1)}, u32[]{:S(2)}, u32[]{:S(2)}) collective-permute-start(bf16[1280,640]{1,0:T(8,128)(2,1)} %all-gather.27.cloned.1.call-done.refs_5_.refs_2_), channel_id=1, source_target_pairs={{0,4},{4,0},{8,12},{12,8},{16,20},{20,16},{24,28},{28,24},{1,5},{5... | collective-permute-start | bytes 4915208 | tf_op jit(solution)/shard_map/ppermute | solution.py:536
  477.6 235.5 %collective-permute-start.15 = (bf16[1280,1280]{1,0:T(8,128)(2,1)}, bf16[1280,1280]{1,0:T(8,128)(2,1)}, u32[]{:S(2)}, u32[]{:S(2)}) collective-permute-start(bf16[1280,1280]{1,0:T(8,128)(2,1)} %all-gather.19.cloned.1.call-done.refs_1_.refs_2_), channel_id=1, source_target_pairs={{0,4},{4,0},{8,12},{12,8},{16,20},{20,16},{24,28},{28,24},{1,5},{5... | collective-permute-start | bytes 9830408 | tf_op jit(solution)/shard_map/ppermute | solution.py:536
  656.8 94.5 %collective-permute-start.13 = (bf16[1,512,1280]{2,1,0:T(8,128)(2,1)}, bf16[1,512,1280]{2,1,0:T(8,128)(2,1)S(1)}, u32[]{:S(2)}, u32[]{:S(2)}) collective-permute-start(bf16[1,512,1280]{2,1,0:T(8,128)(2,1)} %shard_map.600), channel_id=1, source_target_pairs={{0,1},{1,0},{2,3},{3,2},{4,5},{5,4},{6,7},{7,6},{8,9},{9,8},{10,11... | collective-permute-start | bytes 3932168 | tf_op jit(solution)/shard_map/ppermute | solution.py:539
  953.4 833.7 %reduce-scatter.26.cloned.1.call-start = ((), (), s32[]{:S(2)}) async-start(), calls=%async_computation.27 | async-start | bytes 2048000 | tf_op jit(solution)/shard_map/reduce_scatter | solution.py:681
  975.2 94.3 %collective-permute-start.45 = (bf16[1280,1280]{1,0:T(8,128)(2,1)}, bf16[1280,1280]{1,0:T(8,128)(2,1)S(1)}, u32[]{:S(2)}, u32[]{:S(2)}) collective-permute-start(bf16[1280,1280]{1,0:T(8,128)(2,1)} %shard_map.638), channel_id=1, source_target_pairs={{0,4},{4,0},{8,12},{12,8},{16,20},{20,16},{24,28},{28,24},{1,5},{5... | collective-permute-start | bytes 9830408 | tf_op jit(solution)/shard_map/ppermute | solution.py:536
  1011.0 776.1 %reduce-scatter.22.cloned.1.call-start = ((), (), s32[]{:S(2)}) async-start(), calls=%async_computation.25 | async-start | bytes 4096000 | tf_op jit(solution)/shard_map/reduce_scatter | solution.py:681
  1083.3 763.7 %reduce-scatter.16.cloned.1.call-start = ((), (), s32[]{:S(2)}) async-start(), calls=%async_computation.22 | async-start | bytes 4096000 | tf_op jit(solution)/shard_map/reduce_scatter | solution.py:681
  1209.9 637.1 %reduce-scatter.14.cloned.1.call-start = ((), (), s32[]{:S(2)}) async-start(), calls=%async_computation.21 | async-start | bytes 4096000 | tf_op jit(solution)/shard_map/reduce_scatter | solution.py:681
  1333.0 522.9 %reduce-scatter.20.cloned.1.call-start = ((), (), s32[]{:S(2)}) async-start(), calls=%async_computation.24 | async-start | bytes 4096000 | tf_op jit(solution)/shard_map/reduce_scatter | solution.py:681
  1455.2 400.7 %reduce-scatter.18.cloned.1.call-start = ((), (), s32[]{:S(2)}) async-start(), calls=%async_computation.23 | async-start | bytes 4096000 | tf_op jit(solution)/shard_map/reduce_scatter | solution.py:681
  1505.6 83.2 %collective-permute-start.30 = (bf16[2,512,1280]{2,1,0:T(8,128)(2,1)}, bf16[2,512,1280]{2,1,0:T(8,128)(2,1)}, u32[]{:S(2)}, u32[]{:S(2)}) collective-permute-start(bf16[2,512,1280]{2,1,0:T(8,128)(2,1)} %get-tuple-element.93.refs_1_.refs_0_), channel_id=1, source_target_pairs={{0,1},{1,0},{2,3},{3,2},{4,5},{5,4},{6,7},{7,6},{8,9},{9,8},{10,11... | collective-permute-start | bytes 7864328 | tf_op jit(solution)/shard_map/ppermute | solution.py:539
  1563.4 97.0 %collective-permute-start.22 = (bf16[512,2560]{1,0:T(8,128)(2,1)S(1)}, bf16[512,2560]{1,0:T(8,128)(2,1)}, u32[]{:S(2)}, u32[]{:S(2)}) collective-permute-start(bf16[512,2560]{1,0:T(8,128)(2,1)S(1)} %concatenate.193.refs_0_), channel_id=1, source_target_pairs={{0,2},{1,3},{2,0},{3,1},{4,6},{5,7},{6,4},{7,5},{8,10},{9,11},{10,... | collective-permute-start | bytes 7864328 | tf_op jit(solution)/shard_map/ppermute | solution.py:542
  1588.7 279.0 %reduce-scatter.12.cloned.1.call-start = ((), (), s32[]{:S(2)}) async-start(), calls=%async_computation.20 | async-start | bytes 1638400 | tf_op jit(solution)/shard_map/reduce_scatter | solution.py:681
  1670.8 75.5 %collective-permute-start.39 = (bf16[1280,1024]{1,0:T(8,128)(2,1)}, bf16[1280,1024]{1,0:T(8,128)(2,1)}, u32[]{:S(2)}, u32[]{:S(2)}) collective-permute-start(bf16[1280,1024]{1,0:T(8,128)(2,1)} %shard_map.626), channel_id=1, source_target_pairs={{0,4},{4,0},{8,12},{12,8},{16,20},{20,16},{24,28},{28,24},{1,5},{5... | collective-permute-start | bytes 7864328 | tf_op jit(solution)/shard_map/ppermute | solution.py:536
  1699.4 172.8 %reduce-scatter.10.cloned.1.call-start = ((), (), s32[]{:S(2)}) async-start(), calls=%async_computation.19 | async-start | bytes 3276800 | tf_op jit(solution)/shard_map/reduce_scatter | solution.py:681
  (109 other events, 2587.5 us)
Sparse Core Ops, SparseCore 0:
  11.2 62.9 all-gather.10
  75.7 31.1 all-gather.12
  109.1 64.6 all-gather.22
  175.8 64.2 all-gather.20
  241.5 64.2 all-gather.16
  307.8 64.2 all-gather.14
  374.2 36.7 all-gather.26
  413.1 64.4 all-gather.18
  479.7 36.7 all-gather.24
  518.5 36.9 all-gather.28
  953.5 35.5 reduce-scatter.23
  1011.1 35.6 reduce-scatter.25
  1083.4 61.3 reduce-scatter.21
  1210.0 61.2 reduce-scatter.15
  1333.2 61.5 reduce-scatter.13
  1455.3 61.5 reduce-scatter.19
  1588.8 62.4 reduce-scatter.17
  1699.5 31.6 reduce-scatter.11
  1757.3 52.5 reduce-scatter.9
where the time goes:
time: 1920 us; the launch traced here: 1900 us
  waiting for transfers between devices  917 us (48%)
  Pallas kernels  694 us (36%)
  local copies, waits for them, and re-layouts  117 us (6%)
  other arithmetic  114 us (6%)
  starting transfers between devices  42 us (2%)
    ppermute x18, waiting for transfers between devices, to_twin(): return lax.ppermute(x, DP, twins)  607 us
    pallas_call x40, Pallas kernels, fused_dots(): pl.pallas_call(kernel, grid=grid, in_specs=specs, out_specs=[spec for _,...  424 us
    ppermute x11, waiting for transfers between devices, to_row(): return lax.ppermute(x, TENSOR, [(i, i ^ 2) for i in range(4)])  282 us
    pallas_call x8, Pallas kernels, all_rows(): pl.pallas_call(kernel, grid_spec=pltpu.PrefetchScalarGridSpec(num_scalar_...  164 us
    pallas_call x4, Pallas kernels, glue(): pl.pallas_call(body, grid=(rows // tile,), in_specs=[block(x.shape[0]) fo...  42.4 us
  transfers between devices with their start and end apart: 72, of which 25 were waited for; matrix products, arithmetic and copies ran while one was open for 11% of the time, Pallas kernels for 34%

commit v1 on v0

--- a/solution.py
+++ b/solution.py
@@ -672,16 +672,22 @@
             finish,
         )[0]
 
-    def scatter_model(left, rights):
+    def scatter_outer(total):
+        return lax.psum_scatter(total, DP, scatter_dimension=0, tiled=True, axis_index_groups=outer)
+
+    def scatter_model(left, rights, direct=None):
         found = []
-        for right in rights:
+        for j, right in enumerate(rights):
+            if j == direct:
+                far = weight_grad(left, right, 1, [])
+                near = weight_grad(left, right, 0, [])
+                far = to_twin(scatter_outer(far))
+                near = scatter_outer(near)
+                found.append((near.astype(F32) + far.astype(F32)).astype(HALF))
+                continue
             other = to_twin(weight_grad(left, right, 1, []))
             total = weight_grad(left, right, 0, [other])
-            found.append(
-                lax.psum_scatter(
-                    total, DP, scatter_dimension=0, tiled=True, axis_index_groups=outer
-                )
-            )
+            found.append(scatter_outer(total))
         return jnp.concatenate(found, axis=1) if len(found) > 1 else found[0]
 
     q_cols = query_weight.shape[1]
@@ -793,7 +799,9 @@
     )
 
     grad_pieces = spread(ffn_grad)
-    down_wgrad = scatter_model(grad_pieces, [hidden_parts[0], hidden_parts[2], hidden_parts[1]])
+    down_wgrad = scatter_model(
+        grad_pieces, [hidden_parts[0], hidden_parts[2], hidden_parts[1]], direct=2
+    )
 
     def hidden(sums, extras, outs):
         at = 0
@@ -910,12 +918,9 @@
         heads_square,
     )
     decays = (DECAY_RATE,) * 7 + (0.0, 0.0)
-    results = [
-        adam_update(param, grad_item, mean_item, square_item, decay)
-        for param, grad_item, mean_item, square_item, decay in zip(
-            params, grad_shards, means, squares, decays
-        )
-    ]
+    results = []
+    for parts in zip(params, grad_shards, means, squares, decays):
+        results.append(adam_update(*parts))
     updated = tuple((item[0] for item in results))
     new_means = tuple((item[1] for item in results))
     new_squares = tuple((item[2] for item in results))

time: 1920 us -> 1890 us (0.984)
  waiting for transfers between devices: 917 us -> 890 us
    ppermute x18, waiting for transfers between devices: 607 us -> 580 us  [to_twin(): return lax.ppermute(x, DP, twins)]
  transfers between devices with their start and end apart: 72 -> 73, of which waited for: 25 -> 24; matrix products, arithmetic and copies ran while one was open for 11% -> 11% of each run, Pallas kernels for 34% -> 35%
where the time goes in v1:
time: 1890 us; the launch traced here: 1870 us
  waiting for transfers between devices  890 us (47%)
  Pallas kernels  694 us (37%)
  local copies, waits for them, and re-layouts  116 us (6%)
  other arithmetic  115 us (6%)
  starting transfers between devices  42.1 us (2%)
    ppermute x18, waiting for transfers between devices, to_twin(): return lax.ppermute(x, DP, twins)  580 us
    pallas_call x40, Pallas kernels, fused_dots(): pl.pallas_call(kernel, grid=grid, in_specs=specs, out_specs=[spec for _,...  424 us
    ppermute x11, waiting for transfers between devices, to_row(): return lax.ppermute(x, TENSOR, [(i, i ^ 2) for i in range(4)])  282 us
    pallas_call x8, Pallas kernels, all_rows(): pl.pallas_call(kernel, grid_spec=pltpu.PrefetchScalarGridSpec(num_scalar_...  164 us
    pallas_call x4, Pallas kernels, glue(): pl.pallas_call(body, grid=(rows // tile,), in_specs=[block(x.shape[0]) fo...  42.4 us
  transfers between devices with their start and end apart: 73, of which 24 were waited for; matrix products, arithmetic and copies ran while one was open for 11% of the time, Pallas kernels for 35%

profile of v1, /device:TPU:0, one launch (start us, length us, event | category | flops | bytes accessed | tf_op | source)
XLA Modules:
  0.0 1873.2 jit_solution(1173745844318869556)
XLA Ops:
  110.4 36.2 %collective-permute-done = bf16[1280,1152]{0,1:T(8,128)(2,1)} collective-permute-done((bf16[1280,1152]{0,1:T(8,128)(2,1)}, bf16[1280,1152]{0,1:T(8,128)(2,1)}, u32[]{:S(2)}, u32[]{:S(2)}) %collective-permute-start) | collective-permute-done | bytes 2949152 | tf_op jit(solution)/shard_map/ppermute | solution.py:536
  164.7 17.0 shard_map.590
  202.1 13.7 attend.1
  255.1 44.9 %collective-permute-done.4.near = bf16[2,512,1280]{2,1,0:T(8,128)(2,1)S(1)} collective-permute-done((bf16[2,512,1280]{2,1,0:T(8,128)(2,1)}, bf16[2,512,1280]{2,1,0:T(8,128)(2,1)S(1)}, u32[]{:S(2)}, u32[]{:S(2)}) %collective-permute-start.4) | collective-permute-done | bytes 2621472 | tf_op jit(solution)/shard_map/ppermute | solution.py:542
  317.1 54.6 %collective-permute-done.6.refs_2_.refs_4_ = bf16[2,512,1280]{2,1,0:T(8,128)(2,1)} collective-permute-done((bf16[2,512,1280]{2,1,0:T(8,128)(2,1)S(1)}, bf16[2,512,1280]{2,1,0:T(8,128)(2,1)}, u32[]{:S(2)}, u32[]{:S(2)}) %collective-permute-start.6) | collective-permute-done | bytes 2621472 | tf_op jit(solution)/shard_map/ppermute | solution.py:542
  373.3 92.7 %collective-permute-done.16 = bf16[320,640]{1,0:T(8,128)(2,1)S(1)} collective-permute-done((bf16[320,640]{1,0:T(8,128)(2,1)S(1)}, bf16[320,640]{1,0:T(8,128)(2,1)S(1)}, u32[]{:S(2)}, u32[]{:S(2)}) %collective-permute-start.16) | collective-permute-done | bytes 409632 | tf_op jit(solution)/shard_map/ppermute | solution.py:536
  479.0 38.5 %shard_map.597 = (bf16[2048,1280]{1,0:T(8,128)(2,1)}, bf16[2048,1280]{1,0:T(8,128)(2,1)}, bf16[2048,1280]{1,0:T(8,128)(2,1)}) custom-call(bf16[2,512,1280]{2,1,0:T(8,128)(2,1)} %copy-done, bf16[2,512,1280]{2,1,0:T(8,128)(2,1)} %collective-permute-done.5.refs_1_.refs_2_, bf16[2,512,1280]{2,1,0:T(8,128)(2,1)} %collective-permute-done.6.refs_2_.refs_4_, ...), custom_call_target="tpu_custom_call" | custom-call | flops 26843545600 | bytes 23592960 | tf_op jit(solution)/shard_map/pallas_call | solution.py:313
  517.6 22.6 %collective-permute-done.9.refs_7_.refs_13_ = bf16[1280,1280]{1,0:T(8,128)(2,1)} collective-permute-done((bf16[1280,1280]{1,0:T(8,128)(2,1)}, bf16[1280,1280]{1,0:T(8,128)(2,1)}, u32[]{:S(2)}, u32[]{:S(2)}) %collective-permute-start.9) | collective-permute-done | bytes 3276832 | tf_op jit(solution)/shard_map/ppermute | solution.py:536
  540.2 70.2 %collective-permute-done.8.refs_5_.refs_9_ = bf16[1280,1280]{1,0:T(8,128)(2,1)} collective-permute-done((bf16[1280,1280]{1,0:T(8,128)(2,1)}, bf16[1280,1280]{1,0:T(8,128)(2,1)}, u32[]{:S(2)}, u32[]{:S(2)}) %collective-permute-start.8) | collective-permute-done | bytes 3276832 | tf_op jit(solution)/shard_map/ppermute | solution.py:536
  610.4 37.9 %shard_map.596 = (bf16[2048,1280]{1,0:T(8,128)(2,1)}, bf16[2048,1280]{1,0:T(8,128)(2,1)}, bf16[2048,1280]{1,0:T(8,128)(2,1)}) custom-call(bf16[2,512,1280]{2,1,0:T(8,128)(2,1)} %copy-done, bf16[2,512,1280]{2,1,0:T(8,128)(2,1)} %collective-permute-done.5.refs_1_.refs_2_, bf16[2,512,1280]{2,1,0:T(8,128)(2,1)} %collective-permute-done.6.refs_2_.refs_4_, ...), custom_call_target="tpu_custom_call" | custom-call | flops 26843545600 | bytes 23592960 | tf_op jit(solution)/shard_map/pallas_call | solution.py:313
  656.8 56.2 %collective-permute-done.15.refs_1_.refs_3_ = bf16[1280,1280]{1,0:T(8,128)(2,1)} collective-permute-done((bf16[1280,1280]{1,0:T(8,128)(2,1)}, bf16[1280,1280]{1,0:T(8,128)(2,1)}, u32[]{:S(2)}, u32[]{:S(2)}) %collective-permute-start.15) | collective-permute-done | bytes 3276832 | tf_op jit(solution)/shard_map/ppermute | solution.py:536
  792.9 27.6 %collective-permute-done.20.near_b = bf16[1,512,1280]{2,1,0:T(8,128)(2,1)S(1)} collective-permute-done((bf16[1,512,1280]{2,1,0:T(8,128)(2,1)}, bf16[1,512,1280]{2,1,0:T(8,128)(2,1)S(1)}, u32[]{:S(2)}, u32[]{:S(2)}) %collective-permute-start.20) | collective-permute-done | bytes 1310752 | tf_op jit(solution)/shard_map/ppermute | solution.py:542
  832.0 58.1 %collective-permute-done.26.refs_0_.refs_4_ = bf16[2,512,1280]{2,1,0:T(8,128)(2,1)S(1)} collective-permute-done((bf16[2,512,1280]{2,1,0:T(8,128)(2,1)}, bf16[2,512,1280]{2,1,0:T(8,128)(2,1)S(1)}, u32[]{:S(2)}, u32[]{:S(2)}) %collective-permute-start.26) | collective-permute-done | bytes 2621472 | tf_op jit(solution)/shard_map/ppermute | solution.py:542
  936.3 25.1 %collective-permute-done.46.refs_8_ = bf16[1280,640]{1,0:T(8,128)(2,1)S(1)} collective-permute-done((bf16[1280,640]{1,0:T(8,128)(2,1)}, bf16[1280,640]{1,0:T(8,128)(2,1)S(1)}, u32[]{:S(2)}, u32[]{:S(2)}) %collective-permute-start.46) | collective-permute-done | bytes 1638432 | tf_op jit(solution)/shard_map/ppermute | solution.py:536
  971.6 59.2 %collective-permute-done.45.refs_8_ = bf16[1280,1280]{1,0:T(8,128)(2,1)S(1)} collective-permute-done((bf16[1280,1280]{1,0:T(8,128)(2,1)}, bf16[1280,1280]{1,0:T(8,128)(2,1)S(1)}, u32[]{:S(2)}, u32[]{:S(2)}) %collective-permute-start.45) | collective-permute-done | bytes 3276832 | tf_op jit(solution)/shard_map/ppermute | solution.py:536
  1044.6 14.8 shard_map.611
  1059.5 14.7 shard_map.615
  1087.3 70.9 %collective-permute-done.42.refs_8_ = bf16[1280,1280]{1,0:T(8,128)(2,1)S(1)} collective-permute-done((bf16[1280,1280]{1,0:T(8,128)(2,1)}, bf16[1280,1280]{1,0:T(8,128)(2,1)S(1)}, u32[]{:S(2)}, u32[]{:S(2)}) %collective-permute-start.42) | collective-permute-done | bytes 3276832 | tf_op jit(solution)/shard_map/ppermute | solution.py:536
  1212.0 70.1 %collective-permute-done.41.refs_8_ = bf16[1280,1280]{1,0:T(8,128)(2,1)S(1)} collective-permute-done((bf16[1280,1280]{1,0:T(8,128)(2,1)}, bf16[1280,1280]{1,0:T(8,128)(2,1)S(1)}, u32[]{:S(2)}, u32[]{:S(2)}) %collective-permute-start.41) | collective-permute-done | bytes 3276832 | tf_op jit(solution)/shard_map/ppermute | solution.py:536
  1295.9 23.2 %shard_map.616 = bf16[2,512,1280]{2,1,0:T(8,128)(2,1)} custom-call(bf16[1024,1280]{1,0:T(8,128)(2,1)} %get-tuple-element.88.refs_0_.refs_8_.refs_5_.refs_7_, bf16[1280,1280]{1,0:T(8,128)(2,1)} %all-gather.15.cloned.1.call-done.refs_4_.refs_1_, bf16[1024,1280]{1,0:T(8,128)(2,1)} %get-tuple-element.89.refs_2_.refs_10_.refs_5_.refs_7_, ...), custom_call_target="tpu_custom_call" | custom-call | flops 13421772800 | bytes 36700160 | tf_op jit(solution)/shard_map/pallas_call | solution.py:74
  1332.3 22.7 %shard_map.612 = bf16[2,512,1280]{2,1,0:T(8,128)(2,1)} custom-call(bf16[1024,1280]{1,0:T(8,128)(2,1)} %get-tuple-element.82.refs_0_.refs_8_.refs_1_.refs_3_, bf16[1280,1280]{1,0:T(8,128)(2,1)} %all-gather.15.cloned.1.call-done.refs_4_.refs_1_, bf16[1024,1280]{1,0:T(8,128)(2,1)} %get-tuple-element.85.refs_2_.refs_10_.refs_1_.refs_3_, ...), custom_call_target="tpu_custom_call" | custom-call | flops 13421772800 | bytes 36700160 | tf_op jit(solution)/shard_map/pallas_call | solution.py:74
  1356.8 23.2 %shard_map.617 = bf16[2,512,1280]{2,1,0:T(8,128)(2,1)} custom-call(bf16[1024,1280]{1,0:T(8,128)(2,1)} %get-tuple-element.88.refs_0_.refs_8_.refs_5_.refs_7_, bf16[1280,1280]{1,0:T(8,128)(2,1)} %all-gather.15.cloned.1.call-done.refs_4_.refs_1_, bf16[1024,1280]{1,0:T(8,128)(2,1)} %get-tuple-element.89.refs_2_.refs_10_.refs_5_.refs_7_, ...), custom_call_target="tpu_custom_call" | custom-call | flops 13421772800 | bytes 39321600 | tf_op jit(solution)/shard_map/pallas_call | solution.py:74
  1380.7 23.7 %collective-permute-done.44.refs_8_ = bf16[1280,1280]{1,0:T(8,128)(2,1)S(1)} collective-permute-done((bf16[1280,1280]{1,0:T(8,128)(2,1)}, bf16[1280,1280]{1,0:T(8,128)(2,1)S(1)}, u32[]{:S(2)}, u32[]{:S(2)}) %collective-permute-start.44) | collective-permute-done | bytes 3276832 | tf_op jit(solution)/shard_map/ppermute | solution.py:536
  1418.2 23.3 %shard_map.613.mine = f32[2,512,1280]{2,1,0:T(8,128)} custom-call(bf16[1024,1280]{1,0:T(8,128)(2,1)} %get-tuple-element.82.refs_0_.refs_8_.refs_1_.refs_3_, bf16[1280,1280]{1,0:T(8,128)(2,1)} %all-gather.15.cloned.1.call-done.refs_4_.refs_1_, bf16[1024,1280]{1,0:T(8,128)(2,1)} %get-tuple-element.85.refs_2_.refs_10_.refs_1_.refs_3_, ...), custom_call_target="tpu_custom_call" | custom-call | flops 13421772800 | bytes 39321600 | tf_op jit(solution)/shard_map/pallas_call | solution.py:74
  1441.6 13.5 shard_map.618
  1468.9 44.9 %collective-permute-done.31.refs_3_.refs_4_ = bf16[2,512,1280]{2,1,0:T(8,128)(2,1)} collective-permute-done((bf16[2,512,1280]{2,1,0:T(8,128)(2,1)}, bf16[2,512,1280]{2,1,0:T(8,128)(2,1)}, u32[]{:S(2)}, u32[]{:S(2)}) %collective-permute-start.31) | collective-permute-done | bytes 2621472 | tf_op jit(solution)/shard_map/ppermute | solution.py:542
  1552.0 14.2 shard_map.619.do_ref
  1566.2 21.0 %attend_back.1 = (f32[2048,512]{1,0:T(8,128)}, f32[2048,256]{1,0:T(8,128)S(1)}, f32[2048,256]{1,0:T(8,128)}) custom-call(bf16[2048,512]{1,0:T(8,128)(2,1)} %pad_maximum_fusion.4.q_ref, bf16[2048,256]{1,0:T(8,128)(2,1)S(1)} %copy-done.7, bf16[256,2048]{1,0:T(8,128)(2,1)S(1)} %copy-done.9, bf16[2048,256]{1,0:T(8,128)(2,1)S(1)} %copy-done.8, ...), custom_call_target="tpu_custom_call" | custom-call | flops 13421772800 | bytes 15728640 | tf_op jit(solution)/shard_map/attend_back/pallas_call | solution.py:446
  1674.9 14.2 shard_map.609
  1689.0 29.1 %collective-permute-done.47 = bf16[320,640]{1,0:T(8,128)(2,1)S(1)} collective-permute-done((bf16[320,640]{1,0:T(8,128)(2,1)}, bf16[320,640]{1,0:T(8,128)(2,1)S(1)}, u32[]{:S(2)}, u32[]{:S(2)}) %collective-permute-start.47) | collective-permute-done | bytes 409632 | tf_op jit(solution)/shard_map/ppermute | solution.py:536
  1768.5 49.3 %collective-permute-done.49 = f32[84,128]{1,0:T(8,128)S(1)} collective-permute-done((f32[84,128]{1,0:T(8,128)S(1)}, f32[84,128]{1,0:T(8,128)S(1)}, u32[]{:S(2)}, u32[]{:S(2)}) %collective-permute-start.49) | collective-permute-done | bytes 43040 | tf_op jit(solution)/shard_map/ppermute | solution.py:542
  1850.4 15.5 shard_map.625
  (443 shorter events, 714.2 us)
Async XLA Ops:
  11.1 95.9 %all-gather.13.cloned.1.call-start = ((), (), s32[]{:S(2)}) async-start(), calls=%async_computation.11 | async-start | bytes 1638400 | tf_op jit(solution)/shard_map/all_gather | solution.py:630
  11.8 303.2 %all-gather.23.cloned.1.call-start = ((), (), s32[]{:S(2)}) async-start(), calls=%async_computation.16 | async-start | bytes 4096000 | tf_op jit(solution)/shard_map/all_gather | solution.py:630
  13.2 303.3 %all-gather.21.cloned.1.call-start = ((), (), s32[]{:S(2)}) async-start(), calls=%async_computation.15 | async-start | bytes 4096000 | tf_op jit(solution)/shard_map/all_gather | solution.py:630
  14.6 451.5 %all-gather.17.cloned.1.call-start = ((), (), s32[]{:S(2)}) async-start(), calls=%async_computation.13 | async-start | bytes 4096000 | tf_op jit(solution)/shard_map/all_gather | solution.py:630
  15.1 452.4 %all-gather.15.cloned.1.call-start = ((), (), s32[]{:S(2)}) async-start(), calls=%async_computation.12 | async-start | bytes 4096000 | tf_op jit(solution)/shard_map/all_gather | solution.py:630
  15.7 452.5 %all-gather.27.cloned.1.call-start = ((), (), s32[]{:S(2)}) async-start(), calls=%async_computation.18 | async-start | bytes 2048000 | tf_op jit(solution)/shard_map/all_gather | solution.py:630
  106.9 110.8 %collective-permute-start.1 = (bf16[1280,512]{1,0:T(8,128)(2,1)}, bf16[1280,512]{1,0:T(8,128)(2,1)S(1)}, u32[]{:S(2)}, u32[]{:S(2)}) collective-permute-start(bf16[1280,512]{1,0:T(8,128)(2,1)} %all-gather.13.cloned.1.call-done.refs_1_.refs_5_), channel_id=1, source_target_pairs={{0,4},{4,0},{8,12},{12,8},{16,20},{20,16},{24,28},{28,24},{1,5},{5... | collective-permute-start | bytes 3932168 | tf_op jit(solution)/shard_map/ppermute | solution.py:536
  226.0 251.5 %all-gather.19.cloned.1.call-start = ((), (), s32[]{:S(2)}) async-start(), calls=%async_computation.14 | async-start | bytes 4096000 | tf_op jit(solution)/shard_map/all_gather | solution.py:630
  243.4 404.9 %all-gather.25.cloned.1.call-start = ((), (), s32[]{:S(2)}) async-start(), calls=%async_computation.17 | async-start | bytes 2048000 | tf_op jit(solution)/shard_map/all_gather | solution.py:630
  315.0 152.5 %collective-permute-start.11 = (bf16[1280,1280]{1,0:T(8,128)(2,1)}, bf16[1280,1280]{1,0:T(8,128)(2,1)}, u32[]{:S(2)}, u32[]{:S(2)}) collective-permute-start(bf16[1280,1280]{1,0:T(8,128)(2,1)} %all-gather.23.cloned.1.call-done.refs_6_.refs_7_), channel_id=1, source_target_pairs={{0,4},{4,0},{8,12},{12,8},{16,20},{20,16},{24,28},{28,24},{1,5},{5... | collective-permute-start | bytes 9830408 | tf_op jit(solution)/shard_map/ppermute | solution.py:536
  316.5 151.7 %collective-permute-start.10 = (bf16[1280,1280]{1,0:T(8,128)(2,1)}, bf16[1280,1280]{1,0:T(8,128)(2,1)}, u32[]{:S(2)}, u32[]{:S(2)}) collective-permute-start(bf16[1280,1280]{1,0:T(8,128)(2,1)} %all-gather.21.cloned.1.call-done.refs_4_.refs_3_), channel_id=1, source_target_pairs={{0,4},{4,0},{8,12},{12,8},{16,20},{20,16},{24,28},{28,24},{1,5},{5... | collective-permute-start | bytes 9830408 | tf_op jit(solution)/shard_map/ppermute | solution.py:536
  317.1 160.5 %collective-permute-start.5 = (bf16[2,512,1280]{2,1,0:T(8,128)(2,1)S(1)}, bf16[2,512,1280]{2,1,0:T(8,128)(2,1)}, u32[]{:S(2)}, u32[]{:S(2)}) collective-permute-start(bf16[2,512,1280]{2,1,0:T(8,128)(2,1)S(1)} %get-tuple-element.73.refs_0_), channel_id=1, source_target_pairs={{0,1},{1,0},{2,3},{3,2},{4,5},{5,4},{6,7},{7,6},{8,9},{9,8},{10,11... | collective-permute-start | bytes 7864328 | tf_op jit(solution)/shard_map/ppermute | solution.py:539
  371.6 107.4 %collective-permute-start.7 = (bf16[2,512,1280]{2,1,0:T(8,128)(2,1)}, bf16[2,512,1280]{2,1,0:T(8,128)(2,1)}, u32[]{:S(2)}, u32[]{:S(2)}) collective-permute-start(bf16[2,512,1280]{2,1,0:T(8,128)(2,1)} %collective-permute-done.6.refs_2_.refs_4_), channel_id=1, source_target_pairs={{0,1},{1,0},{2,3},{3,2},{4,5},{5,4},{6,7},{7,6},{8,9},{9,8},{10,11... | collective-permute-start | bytes 7864328 | tf_op jit(solution)/shard_map/ppermute | solution.py:539
  371.7 285.1 %all-gather.29.cloned.1.call-start = ((), (), s32[]{:S(2)}) async-start(), calls=%async_computation.19 | async-start | bytes 2048000 | tf_op jit(solution)/shard_map/all_gather | solution.py:630
  371.7 94.3 %collective-permute-start.16 = (bf16[320,640]{1,0:T(8,128)(2,1)S(1)}, bf16[320,640]{1,0:T(8,128)(2,1)S(1)}, u32[]{:S(2)}, u32[]{:S(2)}) collective-permute-start(bf16[320,640]{1,0:T(8,128)(2,1)S(1)} %copy-done.28), channel_id=1, source_target_pairs={{0,4},{4,0},{8,12},{12,8},{16,20},{20,16},{24,28},{28,24},{1,5},{5... | collective-permute-start | bytes 1228808 | tf_op jit(solution)/shard_map/ppermute | solution.py:536
  467.5 142.8 %collective-permute-start.8 = (bf16[1280,1280]{1,0:T(8,128)(2,1)}, bf16[1280,1280]{1,0:T(8,128)(2,1)}, u32[]{:S(2)}, u32[]{:S(2)}) collective-permute-start(bf16[1280,1280]{1,0:T(8,128)(2,1)} %all-gather.15.cloned.1.call-done.refs_4_.refs_1_), channel_id=1, source_target_pairs={{0,4},{4,0},{8,12},{12,8},{16,20},{20,16},{24,28},{28,24},{1,5},{5... | collective-permute-start | bytes 9830408 | tf_op jit(solution)/shard_map/ppermute | solution.py:536
  468.1 1205.3 %reduce-scatter.29.cloned.1.call-start = ((), (), s32[]{:S(2)}) async-start(), calls=%async_computation.29 | async-start | bytes 2048000 | tf_op jit(solution)/shard_map/reduce_scatter | solution.py:676
  468.2 252.3 %collective-permute-start.17 = (bf16[1280,640]{1,0:T(8,128)(2,1)}, bf16[1280,640]{1,0:T(8,128)(2,1)}, u32[]{:S(2)}, u32[]{:S(2)}) collective-permute-start(bf16[1280,640]{1,0:T(8,128)(2,1)} %all-gather.27.cloned.1.call-done.refs_5_.refs_2_), channel_id=1, source_target_pairs={{0,4},{4,0},{8,12},{12,8},{16,20},{20,16},{24,28},{28,24},{1,5},{5... | collective-permute-start | bytes 4915208 | tf_op jit(solution)/shard_map/ppermute | solution.py:536
  477.6 235.4 %collective-permute-start.15 = (bf16[1280,1280]{1,0:T(8,128)(2,1)}, bf16[1280,1280]{1,0:T(8,128)(2,1)}, u32[]{:S(2)}, u32[]{:S(2)}) collective-permute-start(bf16[1280,1280]{1,0:T(8,128)(2,1)} %all-gather.19.cloned.1.call-done.refs_1_.refs_2_), channel_id=1, source_target_pairs={{0,4},{4,0},{8,12},{12,8},{16,20},{20,16},{24,28},{28,24},{1,5},{5... | collective-permute-start | bytes 9830408 | tf_op jit(solution)/shard_map/ppermute | solution.py:536
  656.8 94.5 %collective-permute-start.13 = (bf16[1,512,1280]{2,1,0:T(8,128)(2,1)}, bf16[1,512,1280]{2,1,0:T(8,128)(2,1)S(1)}, u32[]{:S(2)}, u32[]{:S(2)}) collective-permute-start(bf16[1,512,1280]{2,1,0:T(8,128)(2,1)} %shard_map.600), channel_id=1, source_target_pairs={{0,1},{1,0},{2,3},{3,2},{4,5},{5,4},{6,7},{7,6},{8,9},{9,8},{10,11... | collective-permute-start | bytes 3932168 | tf_op jit(solution)/shard_map/ppermute | solution.py:539
  905.2 783.8 %reduce-scatter.27.cloned.1.call-start = ((), (), s32[]{:S(2)}) async-start(), calls=%async_computation.28 | async-start | bytes 2048000 | tf_op jit(solution)/shard_map/reduce_scatter | solution.py:676
  913.9 846.4 %reduce-scatter.25.cloned.1.call-start = ((), (), s32[]{:S(2)}) async-start(), calls=%async_computation.27 | async-start | bytes 2048000 | tf_op jit(solution)/shard_map/reduce_scatter | solution.py:676
  935.7 95.1 %collective-permute-start.45 = (bf16[1280,1280]{1,0:T(8,128)(2,1)}, bf16[1280,1280]{1,0:T(8,128)(2,1)S(1)}, u32[]{:S(2)}, u32[]{:S(2)}) collective-permute-start(bf16[1280,1280]{1,0:T(8,128)(2,1)} %shard_map.638), channel_id=1, source_target_pairs={{0,4},{4,0},{8,12},{12,8},{16,20},{20,16},{24,28},{28,24},{1,5},{5... | collective-permute-start | bytes 9830408 | tf_op jit(solution)/shard_map/ppermute | solution.py:536
  971.5 788.8 %reduce-scatter.23.cloned.1.call-start = ((), (), s32[]{:S(2)}) async-start(), calls=%async_computation.26 | async-start | bytes 4096000 | tf_op jit(solution)/shard_map/reduce_scatter | solution.py:676
  1044.6 775.6 %reduce-scatter.17.cloned.1.call-start = ((), (), s32[]{:S(2)}) async-start(), calls=%async_computation.23 | async-start | bytes 4096000 | tf_op jit(solution)/shard_map/reduce_scatter | solution.py:676
  1172.0 648.2 %reduce-scatter.15.cloned.1.call-start = ((), (), s32[]{:S(2)}) async-start(), calls=%async_computation.22 | async-start | bytes 4096000 | tf_op jit(solution)/shard_map/reduce_scatter | solution.py:676
  1295.9 533.3 %reduce-scatter.21.cloned.1.call-start = ((), (), s32[]{:S(2)}) async-start(), calls=%async_computation.25 | async-start | bytes 4096000 | tf_op jit(solution)/shard_map/reduce_scatter | solution.py:676
  1418.2 411.0 %reduce-scatter.19.cloned.1.call-start = ((), (), s32[]{:S(2)}) async-start(), calls=%async_computation.24 | async-start | bytes 4096000 | tf_op jit(solution)/shard_map/reduce_scatter | solution.py:676
  1526.5 97.2 %collective-permute-start.22 = (bf16[512,2560]{1,0:T(8,128)(2,1)S(1)}, bf16[512,2560]{1,0:T(8,128)(2,1)}, u32[]{:S(2)}, u32[]{:S(2)}) collective-permute-start(bf16[512,2560]{1,0:T(8,128)(2,1)S(1)} %concatenate.193.refs_0_), channel_id=1, source_target_pairs={{0,2},{1,3},{2,0},{3,1},{4,6},{5,7},{6,4},{7,5},{8,10},{9,11},{10,... | collective-permute-start | bytes 7864328 | tf_op jit(solution)/shard_map/ppermute | solution.py:542
  1551.9 288.9 %reduce-scatter.13.cloned.1.call-start = ((), (), s32[]{:S(2)}) async-start(), calls=%async_computation.21 | async-start | bytes 1638400 | tf_op jit(solution)/shard_map/reduce_scatter | solution.py:676
  1634.0 85.4 %collective-permute-start.39 = (bf16[1280,1024]{1,0:T(8,128)(2,1)}, bf16[1280,1024]{1,0:T(8,128)(2,1)}, u32[]{:S(2)}, u32[]{:S(2)}) collective-permute-start(bf16[1280,1024]{1,0:T(8,128)(2,1)} %shard_map.626), channel_id=1, source_target_pairs={{0,4},{4,0},{8,12},{12,8},{16,20},{20,16},{24,28},{28,24},{1,5},{5... | collective-permute-start | bytes 7864328 | tf_op jit(solution)/shard_map/ppermute | solution.py:536
  1662.7 182.8 %reduce-scatter.11.cloned.1.call-start = ((), (), s32[]{:S(2)}) async-start(), calls=%async_computation.20 | async-start | bytes 3276800 | tf_op jit(solution)/shard_map/reduce_scatter | solution.py:676
  (111 other events, 2736.5 us)
Sparse Core Ops, SparseCore 0:
  11.2 62.9 all-gather.10
  75.7 31.1 all-gather.12
  109.1 64.6 all-gather.22
  175.8 64.2 all-gather.20
  241.5 64.2 all-gather.16
  307.8 64.2 all-gather.14
  374.2 36.7 all-gather.26
  413.1 64.4 all-gather.18
  479.7 36.7 all-gather.24
  518.5 36.9 all-gather.28
  905.3 35.4 reduce-scatter.28
  943.0 35.3 reduce-scatter.26
  980.6 35.3 reduce-scatter.24
  1044.7 61.5 reduce-scatter.22
  1172.1 61.5 reduce-scatter.16
  1296.0 61.6 reduce-scatter.14
  1418.3 61.6 reduce-scatter.20
  1552.0 62.5 reduce-scatter.18
  1662.8 31.7 reduce-scatter.12
  1730.4 52.7 reduce-scatter.10
